TPU v7x, 32 devices: a whole 2x2x4 slice. The times are simulated.
32 devices in a mesh: shard: 4 (over z), ctx: 4 (over x, core), tp: 2 (over y).
Axes of the slice: x: 2, y: 2, z: 4, core: 2. Of those that a mesh axis runs over, the one named last changes fastest.
Arguments:
- layer_in: bfloat16 [3072, 2048], P(('shard', 'ctx')), may hold values from -6 to 6
- w_qkv: bfloat16 [6144, 2048], P(('shard', 'ctx'), 'tp'), may hold values from -0.125 to 0.125
- w_out: bfloat16 [2048, 2048], P(('shard', 'ctx'), 'tp'), may hold values from -1.5 to 1.5
- norm_gains: bfloat16 [2048, 4], P(('shard', 'ctx')), may hold values from 0.25 to 1.75
- router: bfloat16 [2048, 16], P(('shard', 'ctx')), may hold values from -0.0625 to 0.0625
- w_gate_up: bfloat16 [16, 2048, 2, 1024], P(('shard', 'ctx'), None, None, 'tp'), may hold values from -0.125 to 0.125
- w_down: bfloat16 [16, 2048, 1024], P(('shard', 'ctx'), None, 'tp'), may hold values from -0.75 to 0.75
- routes: int32 [3072, 8], P(('shard', 'ctx')), may hold values from 0 to 15, all different within a row; in each aligned block of 192 rows (0 to 191, 192 to 383, ...) at most 120 rows name the same one
- lengths: int32 [4, 3], P('shard'), may hold values from 1 to 614, 768 in all within a row
- token_order: int32 [4, 768], P('shard'), may hold values from 0 to 767, each once within a row
- out_grad: bfloat16 [3072, 2048], P(('shard', 'ctx')), may hold values from -6 to 6
Outputs:
- output: bfloat16 [3072, 2048], P(('shard', 'ctx'))
- input_grad: float32 [3072, 2048], P(('shard', 'ctx'))
- qkv_grad: float32 [6144, 2048], P(('shard', 'ctx'), 'tp')
- out_proj_grad: float32 [2048, 2048], P(('shard', 'ctx'), 'tp')
- gains_grad: float32 [2048, 4], P(('shard', 'ctx'))
- router_grad: float32 [2048, 16], P(('shard', 'ctx'))
- gate_up_grad: float32 [16, 2048, 2, 1024], P(('shard', 'ctx'), None, None, 'tp')
- down_grad: float32 [16, 2048, 1024], P(('shard', 'ctx'), None, 'tp')
Inputs may be any that keep to these rules, and one draw needn't show every extreme that they name: `routes`: each row names 8 different experts. Among the 192 rows of one device no expert is named more than 120 times, a bound that some block reaches there. Each row holds the lengths of the 3 sequences of one group; they sum to 768 and the longest is exactly 614. `token_order`: each row is a permutation of the places of its group.
All inputs are finite; a program needn't handle non-finite values.
Results may differ from a plain program's by a relative error of at most 0.017.
Values may be sent and summed in bfloat16 or wider, within the bound.
No kernel may reach another device: no remote copies, remote signals or barrier semaphores. Data moves between devices by JAX's collectives and lax.ppermute only.
A program may use at most 320 MiB of HBM per device.

v0:
```python
import functools
import math

import jax
import jax.numpy as jnp
from jax import lax
from jax.experimental import pallas as pl
from jax.experimental.layout import Layout, with_layout_constraint
from jax.experimental.pallas import tpu as pltpu
from jax.sharding import PartitionSpec as P

HEAD = 128
LANES = 128


norm_eps = 1e-05
rope_base = 10000.0
masked_score = -1e30


def places_info(order_row, length_row):
    seq_ends = jnp.cumsum(length_row)
    seq_starts = seq_ends - length_row
    sequence = jnp.sum((order_row[:, None] >= seq_ends[None, :]).astype(jnp.int32), axis=1)
    picker = jnp.arange(length_row.shape[0], dtype=jnp.int32)[None, :] == sequence[:, None]
    first_place = jnp.sum(jnp.where(picker, seq_starts[None, :], 0), axis=1)
    return (sequence, order_row - first_place)


def rope_tables(place_pos, head_size):
    freq_index = jnp.arange(head_size // 2, dtype=jnp.float32)
    inverse = 1.0 / rope_base ** (freq_index * 2.0 / head_size)
    angle = place_pos.astype(jnp.float32)[:, None] * inverse[None, :]
    cosine = jnp.cos(angle)
    sine = jnp.sin(angle)
    return (jnp.concatenate([cosine, cosine], 1), jnp.concatenate([sine, sine], 1))


def rotate(values_in, cosine, sine):
    half_width = values_in.shape[-1] // 2
    turned = jnp.concatenate([-values_in[..., half_width:], values_in[..., :half_width]], -1)
    return values_in * cosine[:, None, :] + turned * sine[:, None, :]


def rotate_back(grad_in, cosine, sine):
    half_width = grad_in.shape[-1] // 2
    scaled = grad_in * sine[:, None, :]
    return grad_in * cosine[:, None, :] + jnp.concatenate(
        [scaled[..., half_width:], -scaled[..., :half_width]], -1
    )


def swap_tp(values_in):
    return lax.ppermute(values_in, "tp", [(0, 1), (1, 0)])


def swap_ctx(values_in, bit):
    return lax.ppermute(values_in, "ctx", [(i, i ^ bit) for i in range(lax.axis_size("ctx"))])


def shift_shard(values_in, step):
    size = lax.axis_size("shard")
    return lax.ppermute(values_in, "shard", [(i, (i + step) % size) for i in range(size)])


def row_major(values_in):
    return with_layout_constraint(values_in, Layout(major_to_minor=tuple(range(values_in.ndim))))


def add_low(first, *others):
    total = first.astype(jnp.float32)
    for other in others:
        total = total + other.astype(jnp.float32)
    return total


def weight_grad_kernel(sub, count, added, order_ref, rows_ref, raw_ref, *refs):
    step = pl.program_id(0)
    block = order_ref[step]
    outs = refs[1:] if added else refs
    pieces = outs[0].shape[-2] // sub
    totals = []
    for piece in range(pieces):
        granule = block * pieces + piece
        matrix = granule // count
        start = pl.multiple_of((granule % count) * sub, sub)
        total = jnp.dot(
            rows_ref[pl.ds(start, sub), :], raw_ref[matrix], preferred_element_type=jnp.float32
        )
        if added:
            total = total + refs[0][0, piece * sub : (piece + 1) * sub, :].astype(jnp.float32)
        totals.append(total.astype(jnp.bfloat16))
    whole = jnp.concatenate(totals, axis=0)
    if added:
        for position, out in enumerate(outs):

            @pl.when(step == position)
            def _(out=out):
                out[...] = whole
    else:
        outs[0][0] = whole


def weight_grad_blocks(order, rows, raw, block_rows, added=None):
    width, tokens = rows.shape
    columns = raw.shape[2]
    sub = math.gcd(block_rows, width)
    blocks = order.shape[0]
    block_spec = pl.BlockSpec((1, block_rows, columns), lambda i, order: (i, 0, 0))
    in_specs = [
        pl.BlockSpec((width, tokens), lambda i, order: (0, 0)),
        pl.BlockSpec(raw.shape, lambda i, order: (0, 0, 0)),
    ]
    operands = [rows, raw]
    if added is None:
        out_shape = jax.ShapeDtypeStruct((blocks, block_rows, columns), jnp.bfloat16)
        out_specs = block_spec
    else:
        in_specs.append(block_spec)
        operands.append(added)
        out_shape = [jax.ShapeDtypeStruct((block_rows, columns), jnp.bfloat16)] * blocks
        out_specs = [pl.BlockSpec((block_rows, columns), lambda i, order: (0, 0))] * blocks
    return pl.pallas_call(
        functools.partial(weight_grad_kernel, sub, width // sub, added is not None),
        out_shape=out_shape,
        grid_spec=pltpu.PrefetchScalarGridSpec(
            num_scalar_prefetch=1, grid=(blocks,), in_specs=in_specs, out_specs=out_specs
        ),
        cost_estimate=pl.CostEstimate(
            flops=2 * blocks * block_rows * tokens * columns,
            bytes_accessed=2 * blocks * block_rows * columns * len(in_specs),
            transcendentals=0,
        ),
    )(order, *operands)


def reorder_kernel(order_ref, rows_ref, out_ref):
    out_ref[...] = rows_ref[...]


def reorder_blocks(order, rows):
    spec = (1,) + rows.shape[1:]
    return pl.pallas_call(
        reorder_kernel,
        out_shape=jax.ShapeDtypeStruct(rows.shape, rows.dtype),
        grid_spec=pltpu.PrefetchScalarGridSpec(
            num_scalar_prefetch=1,
            grid=(rows.shape[0],),
            in_specs=[pl.BlockSpec(spec, lambda i, order: (order[i], 0, 0))],
            out_specs=pl.BlockSpec(spec, lambda i, order: (i, 0, 0)),
        ),
        cost_estimate=pl.CostEstimate(
            flops=0, bytes_accessed=2 * rows.size * rows.dtype.itemsize, transcendentals=0
        ),
    )(order, rows)


TILE = 256


def expert_in_kernel(experts, index_ref, rows_ref, grads_ref, *refs):
    f32, bf16 = jnp.float32, jnp.bfloat16
    weights, (act_ref, dgate_ref, dup_ref, score_ref) = refs[:6], refs[6:]
    width = weights[0].shape[0]
    tile = pl.program_id(0)

    def through(gate_ref, up_ref, back_ref):
        extra = rows_ref[:, width:].astype(f32)
        column = lax.broadcasted_iota(jnp.int32, extra.shape, 1)
        mine_in = (column % experts == index_ref[0]) & (column < 3 * experts)
        gate_col = jnp.sum(jnp.where(mine_in, extra, 0.0), axis=1, keepdims=True)
        rows = rows_ref[:, :width]
        gate_val = jnp.dot(rows, gate_ref[...], preferred_element_type=f32)
        up_val = jnp.dot(rows, up_ref[...], preferred_element_type=f32)
        hidden_raw = jnp.dot(grads_ref[0], back_ref[...], preferred_element_type=f32)
        gate_sig = jax.nn.sigmoid(gate_val)
        gate_act = gate_val * gate_sig
        hidden_act = gate_act * up_val
        act_ref[...] = (gate_col * hidden_act).astype(bf16)
        hidden_grad = gate_col * hidden_raw
        dgate = hidden_grad * up_val * gate_sig * (1.0 + gate_val * (1.0 - gate_sig))
        dgate_ref[...] = dgate.astype(bf16)
        dup_ref[...] = (hidden_grad * gate_act).astype(bf16)
        score = hidden_act * hidden_raw
        lanes = score[:, :LANES]
        for start in range(LANES, TILE, LANES):
            lanes = lanes + score[:, start : start + LANES]

        @pl.when(tile == 0)
        def _():
            score_ref[...] = lanes

        @pl.when(tile > 0)
        def _():
            score_ref[...] += lanes

    side = pl.num_programs(0) // 2

    @pl.when(tile < side)
    def _():
        through(*weights[:3])

    @pl.when(tile >= side)
    def _():
        through(*weights[3:])


def expert_in(index, rows, grads, group, own, other, experts):
    count, columns = rows.shape
    width, hidden = own[1].shape
    side = hidden // TILE

    def tiles(shift, base):
        return pl.BlockSpec(
            (width, TILE), lambda h, index: (0, base + jnp.clip(h - shift, 0, side - 1))
        )

    weight_specs = [tiles(shift, base) for shift in (0, side) for base in (0, side, 0)]
    wide = pl.BlockSpec((count, TILE), lambda h, index: (0, h))
    return pl.pallas_call(
        functools.partial(expert_in_kernel, experts),
        out_shape=[jax.ShapeDtypeStruct((count, 2 * hidden), jnp.bfloat16)] * 3
        + [jax.ShapeDtypeStruct((count, LANES), jnp.float32)],
        grid_spec=pltpu.PrefetchScalarGridSpec(
            num_scalar_prefetch=1,
            grid=(2 * side,),
            in_specs=[
                pl.BlockSpec((count, columns), lambda h, index: (0, 0)),
                pl.BlockSpec((1, count, width), lambda h, index: (group, 0, 0)),
            ]
            + weight_specs,
            out_specs=[wide, wide, wide, pl.BlockSpec((count, LANES), lambda h, index: (0, 0))],
        ),
        cost_estimate=pl.CostEstimate(
            flops=12 * count * width * hidden,
            bytes_accessed=12 * width * hidden,
            transcendentals=2 * count * hidden,
        ),
    )(index, rows, grads, own[0], own[0], own[1], other[0], other[0], other[1])


def expert_out_kernel(experts, added, index_ref, act_ref, dgate_ref, dup_ref, score_ref, *refs):
    f32, bf16 = jnp.float32, jnp.bfloat16
    down_own, pair_own, down_other, pair_other = refs[:4]
    outs = refs[5:] if added else refs[4:]
    hidden = down_own.shape[1]
    half = outs[0].shape[0]
    step = pl.program_id(0)
    side = pl.num_programs(0) // 2

    def times(rows, weights):
        return lax.dot_general(
            rows, weights, (((1,), (1,)), ((), ())), preferred_element_type=f32
        )

    def put(total):
        if added:
            total = total + refs[4][...].astype(f32)
        total = total.astype(bf16)
        for piece, out in enumerate(outs):
            out[...] = total[piece * half : (piece + 1) * half, :]

    @pl.when(step < side)
    def _():
        put(
            times(act_ref[:, :hidden], down_own[...])
            + times(act_ref[:, hidden:], down_other[...])
        )

    @pl.when((step >= side) & (step < 2 * side))
    def _():
        put(
            times(dgate_ref[:, :hidden], pair_own[:, :hidden])
            + times(dup_ref[:, :hidden], pair_own[:, hidden:])
            + times(dgate_ref[:, hidden:], pair_other[:, :hidden])
            + times(dup_ref[:, hidden:], pair_other[:, hidden:])
        )

    @pl.when(step == 2 * side)
    def _():
        score = jnp.sum(score_ref[...], axis=1, keepdims=True)
        high = score.astype(bf16).astype(f32)
        spot = lax.broadcasted_iota(jnp.int32, (score.shape[0], TILE), 1)
        rest = jnp.where(spot == index_ref[0] + experts, score - high, 0.0)
        put(jnp.where(spot == index_ref[0], high, rest))


def expert_out(index, act, dgate, dup, score, own, other, experts, pieces, added=None):
    count = act.shape[0]
    width, hidden = own[1].shape
    side = width // TILE
    total = (2 * side + 1) * TILE
    whole = pl.BlockSpec((count, 2 * hidden), lambda n, index: (0, 0))
    wide = pl.BlockSpec((count, TILE), lambda n, index: (0, n))
    down_spec = pl.BlockSpec((TILE, hidden), lambda n, index: (jnp.minimum(n, side - 1), 0))
    pair_spec = pl.BlockSpec(
        (TILE, 2 * hidden), lambda n, index: (jnp.clip(n - side, 0, side - 1), 0)
    )
    in_specs = [
        whole,
        whole,
        whole,
        pl.BlockSpec((count, LANES), lambda n, index: (0, 0)),
        down_spec,
        pair_spec,
        down_spec,
        pair_spec,
    ]
    operands = [act, dgate, dup, score, own[1], own[0], other[1], other[0]]
    if added is not None:
        in_specs.append(wide)
        operands.append(added)
    rows = count // pieces
    return pl.pallas_call(
        functools.partial(expert_out_kernel, experts, added is not None),
        out_shape=[jax.ShapeDtypeStruct((rows, total), jnp.bfloat16)] * pieces,
        grid_spec=pltpu.PrefetchScalarGridSpec(
            num_scalar_prefetch=1,
            grid=(2 * side + 1,),
            in_specs=in_specs,
            out_specs=[pl.BlockSpec((rows, TILE), lambda n, index: (0, n))] * pieces,
        ),
        cost_estimate=pl.CostEstimate(
            flops=12 * count * width * hidden,
            bytes_accessed=12 * width * hidden + 4 * count * total,
            transcendentals=0,
        ),
    )(index, *operands)


def join_halves(mine, other, first_is_mine):
    top = jnp.where(first_is_mine, mine, other)
    bottom = jnp.where(first_is_mine, other, mine)
    return jnp.concatenate([top, bottom], axis=0)


def split_three(values_in):
    high = values_in.astype(jnp.bfloat16)
    rest = values_in - high.astype(jnp.float32)
    middle = rest.astype(jnp.bfloat16)
    low = (rest - middle.astype(jnp.float32)).astype(jnp.bfloat16)
    return [high, middle, low]


def local(
    layer_in,
    w_qkv,
    w_out,
    norm_gains,
    router,
    w_gate_up,
    w_down,
    routes,
    lengths,
    token_order,
    out_grad,
):
    bf16, f32 = jnp.bfloat16, jnp.float32
    highest = lax.Precision.HIGHEST
    tokens, width = layer_in.shape
    experts = router.shape[1]
    hidden = w_down.shape[2]
    half = tokens // 2
    owners = ("shard", "ctx")
    tp_index = lax.axis_index("tp")
    ctx_index = lax.axis_index("ctx")
    ctx_size = lax.axis_size("ctx")
    expert_index = lax.axis_index("shard") * ctx_size + ctx_index
    first_is_mine = tp_index == 0
    my_row = tp_index * half
    other_row = (1 - tp_index) * half

    def my_rows(values_in):
        return lax.dynamic_slice_in_dim(values_in, my_row, half)

    def other_rows(values_in):
        return lax.dynamic_slice_in_dim(values_in, other_row, half)

    small_all = lax.all_gather(
        jnp.concatenate([norm_gains, router], axis=1), owners, axis=0, tiled=True
    )
    qkv_all = lax.all_gather(w_qkv, owners, axis=0, tiled=True)
    out_all = lax.all_gather(w_out, owners, axis=0, tiled=True)
    grad_half = my_rows(out_grad)
    grad_rows = lax.all_gather(grad_half, owners, axis=0, tiled=True)
    pair_own = jnp.concatenate([w_gate_up[0, :, 0], w_gate_up[0, :, 1]], axis=1)
    pair_other = swap_tp(pair_own)

    def hidden_part(which, index):
        return which[:, index * hidden : (index + 1) * hidden]

    half_width = qkv_all.shape[1]
    full_heads = half_width * lax.axis_size("tp")
    head_count = half_width // HEAD
    gains_f = small_all[:, :4].astype(f32)
    router_f = small_all[:, 4:].astype(f32)
    gain_in = gains_f[:, 0]
    gain_mid = gains_f[:, 1]
    gain_q = lax.dynamic_slice_in_dim(gains_f[:, 2], tp_index * half_width, half_width)
    gain_k = lax.dynamic_slice_in_dim(gains_f[:, 3], tp_index * half_width, half_width)
    score_scale = HEAD ** (-0.5)
    seq_all, pos_all = places_info(token_order[0], lengths[0])

    def ctx_rows(table, index):
        return lax.dynamic_slice_in_dim(table, index * tokens, tokens)

    seq_mine, pos_mine = ctx_rows(seq_all, ctx_index), ctx_rows(pos_all, ctx_index)
    key_order = [ctx_index ^ step for step in range(ctx_size)]
    seq_keys = jnp.concatenate([ctx_rows(seq_all, i) for i in key_order])
    pos_keys = jnp.concatenate([ctx_rows(pos_all, i) for i in key_order])
    cosine, sine = rope_tables(pos_mine, HEAD)
    visible = (seq_mine[:, None] == seq_keys[None, :]) & (pos_keys[None, :] <= pos_mine[:, None])

    layer_f = layer_in.astype(f32)
    rate_in = lax.rsqrt(jnp.mean(layer_f * layer_f, axis=-1, keepdims=True) + norm_eps)
    in_hat = layer_f * rate_in
    in_low = row_major((in_hat * gain_in).astype(bf16))
    qkv_mats = qkv_all.reshape(3, width, half_width)
    q_raw, k_raw, v_raw = (
        jnp.dot(in_low, qkv_mats[j], preferred_element_type=f32) for j in range(3)
    )
    v_low = v_raw.astype(bf16)
    square_q, square_k = lax.psum(
        (jnp.sum(q_raw * q_raw, axis=1), jnp.sum(k_raw * k_raw, axis=1)), "tp"
    )
    down_own = lax.optimization_barrier((w_down[0], square_q))[0]
    down_other = swap_tp(down_own)
    own_weights, other_weights = (pair_own, w_down[0]), (pair_other, down_other)
    rate_q = lax.rsqrt(square_q / full_heads + norm_eps)[:, None]
    rate_k = lax.rsqrt(square_k / full_heads + norm_eps)[:, None]
    q_hat = q_raw * rate_q
    k_hat = k_raw * rate_k
    q_low = rotate((q_hat * gain_q).reshape(tokens, head_count, HEAD), cosine, sine).astype(bf16)
    k_low = (
        rotate((k_hat * gain_k).reshape(tokens, head_count, HEAD), cosine, sine)
        .astype(bf16)
        .reshape(tokens, half_width)
    )

    def gather_ctx(block):
        far = swap_ctx(block, 2)
        return jnp.concatenate([block, swap_ctx(block, 1), far, swap_ctx(far, 1)], axis=0)

    group_len = tokens * ctx_size
    value_heads = gather_ctx(v_low).reshape(group_len, head_count, HEAD)
    key_heads = gather_ctx(k_low).reshape(group_len, head_count, HEAD)
    scores = jnp.einsum("qhd,khd->hqk", q_low, key_heads, preferred_element_type=f32) * score_scale
    scores = jnp.where(visible[None], scores, masked_score)
    row_max = jnp.max(scores, axis=-1, keepdims=True)
    shifted = jnp.exp(scores - row_max)
    row_sum = jnp.sum(shifted, axis=-1, keepdims=True)
    weights = shifted / row_sum
    log_total = row_max + jnp.log(row_sum)
    mixed = jnp.einsum(
        "hqk,khd->qhd", weights.astype(bf16), value_heads, preferred_element_type=f32
    )
    mixed_low = mixed.reshape(tokens, half_width).astype(bf16)
    attn_part = lax.dot_general(
        mixed_low, out_all, (((1,), (1,)), ((), ())), preferred_element_type=f32
    )
    attn_part = row_major(attn_part)
    attn = my_rows(attn_part) + swap_tp(other_rows(attn_part).astype(bf16)).astype(f32)

    resid = my_rows(layer_f) + attn
    rate_mid = lax.rsqrt(jnp.mean(resid * resid, axis=-1, keepdims=True) + norm_eps)
    mid_hat = resid * rate_mid
    mid_norm = mid_hat * gain_mid
    logits = jnp.dot(mid_norm, router_f, precision=highest)
    expert_ids = jnp.arange(experts, dtype=jnp.int32)
    chosen = jnp.any(my_rows(routes)[:, :, None] == expert_ids[None, None, :], axis=1)
    logits_max = jnp.max(jnp.where(chosen, logits, -jnp.inf), axis=-1, keepdims=True)
    gates = jnp.where(chosen, jnp.exp(jnp.where(chosen, logits - logits_max, 0.0)), 0.0)
    gates = gates / jnp.sum(gates, axis=-1, keepdims=True)

    def padded(parts):
        columns = sum(part.shape[1] for part in parts)
        rest = -columns % LANES
        if rest:
            parts = parts + [jnp.zeros((parts[0].shape[0], rest), parts[0].dtype)]
        return jnp.concatenate(parts, axis=1)

    shards = lax.axis_size("shard")
    shard_index = lax.axis_index("shard")
    steps = range(shards)

    def block_of(step, far, side):
        return ((shard_index + shards - step) % shards) * ctx_size + (
            ctx_index ^ (2 * far + side)
        )

    mid_block = row_major(padded([mid_norm.astype(bf16)] + split_three(gates)))
    near_blocks = [mid_block] + [shift_shard(mid_block, step) for step in steps[1:]]
    far_blocks = [swap_ctx(block, 2) for block in near_blocks]
    near_group = row_major(jnp.concatenate(near_blocks, axis=0))
    far_group = row_major(jnp.concatenate(far_blocks, axis=0))
    mid_groups = [
        [near_group, swap_ctx(near_group, 1)],
        [far_group, swap_ctx(far_group, 1)],
    ]
    turn_order = jnp.stack(
        [block_of(step, far, side) for far in range(2) for side in range(2) for step in steps]
    ).astype(jnp.int32)
    grad_groups = reorder_blocks(turn_order, grad_rows.reshape(-1, half, width)).reshape(
        4, shards * half, width
    )
    index = expert_index.astype(jnp.int32).reshape(1)
    inside = {
        (far, side): expert_in(
            index, mid_groups[far][side], grad_groups, 2 * far + side, own_weights, other_weights, experts
        )
        for far in range(2)
        for side in range(2)
    }

    def sum_side(far):
        sent = expert_out(index, *inside[far, 1], own_weights, other_weights, experts, 1)[0]
        return expert_out(
            index,
            *inside[far, 0],
            own_weights,
            other_weights,
            experts,
            shards,
            swap_ctx(sent, 1),
        )

    far_sums = sum_side(1)
    far_arrived = [swap_ctx(far_sums[step], 2) for step in steps]
    near_sums = sum_side(0)
    block_sums = [add_low(mine, other) for mine, other in zip(near_sums, far_arrived)]
    step_arrived = [
        shift_shard(block_sums[step].astype(bf16), -step) for step in steps[1:]
    ]
    block_total = row_major(add_low(block_sums[0], *step_arrived))

    pairs = [(far, side) for far in range(2) for side in range(2)]
    mid_all = jnp.concatenate([mid_groups[far][side][:, :width] for far, side in pairs], axis=0)
    act_all, dgate_all, dup_all = (
        jnp.concatenate([inside[pair][which] for pair in pairs], axis=0) for which in range(3)
    )
    grad_all = grad_groups.reshape(-1, width)

    def over_tokens(rows, columns):
        return lax.dot_general(
            rows, columns, (((0,), (0,)), ((), ())), preferred_element_type=f32
        )

    pair_rows = jnp.concatenate(
        [hidden_part(dgate_all, 1), hidden_part(dup_all, 1)], axis=1
    )
    pair_sent = over_tokens(mid_all, pair_rows).astype(bf16)
    pair_arrived = swap_tp(pair_sent)
    gate_up_grad = jnp.stack(
        [
            over_tokens(mid_all, hidden_part(which, 0))
            + hidden_part(pair_arrived, position).astype(f32)
            for position, which in enumerate((dgate_all, dup_all))
        ],
        axis=1,
    )[None]
    down_sent = over_tokens(grad_all, hidden_part(act_all, 1)).astype(bf16)

    mixture = block_total[:, :width]
    mid_grad = block_total[:, width : 2 * width]
    scores_in = block_total[:, 2 * width :]
    score_total = scores_in[:, :experts] + scores_in[:, experts : 2 * experts]
    output_half = (resid + mixture).astype(bf16)
    output = join_halves(output_half, swap_tp(output_half), first_is_mine)
    logit_grad = gates * (score_total - jnp.sum(gates * score_total, axis=1, keepdims=True))
    router_grad = lax.dot_general(
        logit_grad, mid_norm, (((0,), (0,)), ((), ())), precision=highest
    )
    mid_grad = mid_grad + lax.dot_general(
        logit_grad, router_f, (((1,), (1,)), ((), ())), precision=highest
    )
    mid_scaled = gain_mid * mid_grad
    resid_grad = grad_half.astype(f32) + rate_mid * (
        mid_scaled - mid_hat * jnp.mean(mid_hat * mid_scaled, axis=-1, keepdims=True)
    )
    gain_mid_grad = jnp.sum(mid_grad * mid_hat, axis=0, keepdims=True)
    attn_half = resid_grad.astype(bf16)
    attn_low = join_halves(attn_half, swap_tp(attn_half), first_is_mine)
    out_proj_grad = lax.dot_general(
        attn_low, mixed_low, (((0,), (0,)), ((), ())), preferred_element_type=f32
    ).astype(bf16)
    out_owned = lax.psum_scatter(out_proj_grad, owners, scatter_dimension=0, tiled=True)
    out_owned = out_owned.astype(f32)
    mixed_grad = (
        jnp.dot(attn_low, out_all, preferred_element_type=f32)
        .astype(bf16)
        .reshape(tokens, head_count, HEAD)
    )
    again = jnp.einsum("qhd,khd->hqk", q_low, key_heads, preferred_element_type=f32) * score_scale
    again = jnp.where(visible[None], again, masked_score)
    weights_again = jnp.exp(again - log_total)
    weights_low = weights_again.astype(bf16)
    weight_grad = jnp.einsum("qhd,khd->hqk", mixed_grad, value_heads, preferred_element_type=f32)
    score_grad = weights_again * (
        weight_grad - jnp.sum(weights_again * weight_grad, axis=-1, keepdims=True)
    )
    score_low = score_grad.astype(bf16)
    q_grad = (
        jnp.einsum("hqk,khd->qhd", score_low, key_heads, preferred_element_type=f32) * score_scale
    )
    k_part = (
        jnp.einsum("hqk,qhd->khd", score_low, q_low, preferred_element_type=f32) * score_scale
    )
    v_part = jnp.einsum("hqk,qhd->khd", weights_low, mixed_grad, preferred_element_type=f32)

    kv_part = jnp.concatenate(
        [
            part.reshape(ctx_size, tokens, half_width).astype(bf16)
            for part in (k_part, v_part)
        ],
        axis=2,
    )
    kv_arrived = swap_ctx(jnp.stack([kv_part[1], kv_part[3]]), 1)
    kv_far = add_low(kv_part[2], kv_arrived[1]).astype(bf16)
    kv_grad = add_low(kv_part[0], kv_arrived[0], swap_ctx(kv_far, 2))
    k_grad, v_grad = kv_grad[:, :half_width], kv_grad[:, half_width:]
    q_in = rotate_back(q_grad, cosine, sine).reshape(tokens, half_width)
    k_in = rotate_back(k_grad.reshape(tokens, head_count, HEAD), cosine, sine).reshape(
        tokens, half_width
    )
    q_scaled = gain_q * q_in
    k_scaled = gain_k * k_in
    inner_q, inner_k = lax.psum(
        (jnp.sum(q_scaled * q_hat, axis=1), jnp.sum(k_scaled * k_hat, axis=1)), "tp"
    )
    down_sent = lax.optimization_barrier((down_sent, inner_q))[0]
    down_arrived = swap_tp(down_sent)
    down_grad = (over_tokens(grad_all, hidden_part(act_all, 0)) + down_arrived.astype(f32))[None]
    q_raw_grad = rate_q * (q_scaled - q_hat * (inner_q / full_heads)[:, None])
    k_raw_grad = rate_k * (k_scaled - k_hat * (inner_k / full_heads)[:, None])
    raw_grads = [q_raw_grad.astype(bf16), k_raw_grad.astype(bf16), v_grad.astype(bf16)]
    raw_stack = jnp.stack(raw_grads)
    in_turned = in_low.T
    block_rows = w_qkv.shape[0]

    def grad_blocks(far, side, added=None):
        order = jnp.stack(
            [
                ((shard_index + step) % shards) * ctx_size + (ctx_index ^ (2 * far + side))
                for step in steps
            ]
        ).astype(jnp.int32)
        return weight_grad_blocks(order, in_turned, raw_stack, block_rows, added)

    far_grads = grad_blocks(1, 0, swap_ctx(grad_blocks(1, 1), 1))
    far_grads_in = [swap_ctx(far_grads[step], 2) for step in steps]
    near_grads = grad_blocks(0, 0, swap_ctx(grad_blocks(0, 1), 1))
    step_grads = [add_low(near_grads[step], far_grads_in[step]) for step in steps]
    step_grads_in = [shift_shard(step_grads[step].astype(bf16), step) for step in steps[1:]]
    qkv_owned = add_low(step_grads[0], *step_grads_in)
    norm_part = sum(
        lax.dot_general(raw, mat, (((1,), (1,)), ((), ())), preferred_element_type=f32)
        for raw, mat in zip(raw_grads, (qkv_mats[0], qkv_mats[1], qkv_mats[2]))
    )
    norm_arrived = swap_tp(other_rows(norm_part).astype(bf16))
    in_norm_grad = my_rows(norm_part) + norm_arrived.astype(f32)
    in_hat_half = my_rows(in_hat)
    in_scaled = gain_in * in_norm_grad
    input_half = resid_grad + my_rows(rate_in) * (
        in_scaled - in_hat_half * jnp.mean(in_hat_half * in_scaled, axis=-1, keepdims=True)
    )
    input_grad = join_halves(input_half, swap_tp(input_half), first_is_mine)
    gain_in_grad = jnp.sum(in_norm_grad * in_hat_half, axis=0, keepdims=True)
    gain_pair = jnp.stack([jnp.sum(q_in * q_hat, axis=0), jnp.sum(k_in * k_hat, axis=0)], axis=0)
    qk_gain_part = lax.dynamic_update_slice(
        jnp.zeros((2, width), f32), gain_pair, (0, tp_index * half_width)
    )
    everyone = ("shard", "ctx", "tp")
    small_total = lax.psum(
        jnp.concatenate([gain_in_grad, gain_mid_grad, qk_gain_part, router_grad], axis=0),
        everyone,
    )
    small_owned = lax.dynamic_slice_in_dim(
        small_total, expert_index * norm_gains.shape[0], norm_gains.shape[0], axis=1
    ).T
    return (
        output,
        input_grad,
        qkv_owned,
        out_owned,
        small_owned[:, :4],
        small_owned[:, 4:],
        gate_up_grad,
        down_grad,
    )


def solution(mesh):
    in_specs = (
        P(("shard", "ctx"), None),
        P(("shard", "ctx"), "tp"),
        P(("shard", "ctx"), "tp"),
        P(("shard", "ctx"), None),
        P(("shard", "ctx"), None),
        P(("shard", "ctx"), None, None, "tp"),
        P(("shard", "ctx"), None, "tp"),
        P(("shard", "ctx"), None),
        P("shard", None),
        P("shard", None),
        P(("shard", "ctx"), None),
    )
    out_specs = (
        P(("shard", "ctx"), None),
        P(("shard", "ctx"), None),
        P(("shard", "ctx"), "tp"),
        P(("shard", "ctx"), "tp"),
        P(("shard", "ctx"), None),
        P(("shard", "ctx"), None),
        P(("shard", "ctx"), None, None, "tp"),
        P(("shard", "ctx"), None, "tp"),
    )

    return jax.shard_map(local, mesh=mesh, in_specs=in_specs, out_specs=out_specs, check_vma=False)
```

profile of v0, /device:TPU:0, one launch (start us, length us, event | category | flops | bytes accessed | tf_op | source)
XLA Modules:
  0.0 954.4 jit_solution(6428378157434527389)
XLA Ops:
  12.7 24.2 %all_gather.12 = bf16[2048,20]{0,1:T(8,128)(2,1)S(1)} all-gather(bf16[128,20]{0,1:T(8,128)(2,1)S(1)} %pad_maximum_fusion.13), channel_id=1, replica_groups=mesh['shard'=4,'ctx'=4,'tp'=2] {'shard','ctx'}, dimensions={0}, use_global_device_ids=true | all-gather | bytes 87040 | tf_op jit(solution)/shard_map/all_gather | solution.py:379
  39.4 10.2 %fusion.100 = (bf16[1,2048,1,512]{3,2,1,0:T(2,128)(2,1)}, bf16[1,2048,1,512]{3,2,1,0:T(2,128)(2,1)}) fusion(bf16[1,2048,2,512]{3,2,1,0:T(2,128)(2,1)} %param.16), kind=kLoop, calls=%fused_computation.233 | loop fusion | bytes 8388608 | tf_op jit(solution)/shard_map/slice | solution.py:386
  51.0 7.0 copy_bitcast_fusion
  58.1 55.7 %all-gather.4.cloned.1.call-done = bf16[6144,1024]{1,0:T(8,128)(2,1)} async-done(((bf16[384,1024]{1,0:T(8,128)(2,1)}), bf16[6144,1024]{1,0:T(8,128)(2,1)}) %all-gather.4.cloned.1.call-update) | async-done | bytes 12582928 | tf_op jit(solution)/shard_map/all_gather | solution.py:382
  120.7 5.5 all-reduce.1
  134.6 6.3 collective-permute-done.4
  141.0 14.2 %collective-permute-done.1 = bf16[192,1024]{1,0:T(8,128)(2,1)S(1)} collective-permute-done((bf16[192,1024]{1,0:T(8,128)(2,1)S(1)}, bf16[192,1024]{1,0:T(8,128)(2,1)S(1)}, u32[]{:S(2)}, u32[]{:S(2)}) %collective-permute-start.1) | collective-permute-done | bytes 393248 | tf_op jit(solution)/shard_map/ppermute | solution.py:58
  162.0 8.3 all-gather.6.cloned.1.call-done
  170.3 4.0 fusion.70
  181.1 5.4 collective-permute-done.6
  197.4 12.5 %collective-permute-done.7 = bf16[96,2176]{1,0:T(8,128)(2,1)S(1)} collective-permute-done((bf16[96,2176]{1,0:T(8,128)(2,1)}, bf16[96,2176]{1,0:T(8,128)(2,1)S(1)}, u32[]{:S(2)}, u32[]{:S(2)}) %collective-permute-start.7) | collective-permute-done | bytes 417824 | tf_op jit(solution)/shard_map/ppermute | solution.py:63
  211.5 29.8 %collective-permute-done.8 = bf16[96,2176]{1,0:T(8,128)(2,1)S(1)} collective-permute-done((bf16[96,2176]{1,0:T(8,128)(2,1)}, bf16[96,2176]{1,0:T(8,128)(2,1)S(1)}, u32[]{:S(2)}, u32[]{:S(2)}) %collective-permute-start.8) | collective-permute-done | bytes 417824 | tf_op jit(solution)/shard_map/ppermute | solution.py:63
  244.9 8.9 collective-permute-done.16
  254.6 6.1 collective-permute-done.17
  264.0 11.6 %shard_map.170 = bf16[16,96,2048]{2,1,0:T(8,128)(2,1)} custom-call(s32[16]{0:T(128)} %stack.136.order_ref, bf16[16,96,2048]{2,1,0:T(8,128)(2,1)} %bitcast.215), custom_call_target="tpu_custom_call" | custom-call | bytes 12582912 | tf_op jit(solution)/shard_map/pallas_call | solution.py:143
  276.4 44.2 %collective-permute-done.11.refs_5_.refs_2_ = bf16[2048,512]{1,0:T(8,128)(2,1)} collective-permute-done((bf16[2048,512]{1,0:T(8,128)(2,1)S(1)}, bf16[2048,512]{1,0:T(8,128)(2,1)}, u32[]{:S(2)}, u32[]{:S(2)}) %collective-permute-start.11) | collective-permute-done | bytes 2097184 | tf_op jit(solution)/shard_map/ppermute | solution.py:54
  320.6 11.7 %shard_map.176 = (bf16[384,1024]{1,0:T(8,128)(2,1)}, bf16[384,1024]{1,0:T(8,128)(2,1)}, bf16[384,1024]{1,0:T(8,128)(2,1)}, f32[384,128]{1,0:T(8,128)}) custom-call(s32[1]{0:T(128)} %bitcast.8.index_ref, bf16[384,2176]{1,0:T(8,128)(2,1)} %collective-permute-done.18.rows_ref, bf16[4,384,2048]{2,1,0:T(8,128)(2,1)} %bitcast.189, ...), custom_call_target="tpu_custom_call" | custom-call | flops 4831838208 | bytes 12582912 | tf_op jit(solution)/shard_map/pallas_call | solution.py:220
  332.3 16.6 %shard_map.177 = bf16[384,4352]{1,0:T(8,128)(2,1)} custom-call(s32[1]{0:T(128)} %bitcast.8.index_ref, bf16[384,1024]{1,0:T(8,128)(2,1)} %get-tuple-element.56.act_ref, bf16[384,1024]{1,0:T(8,128)(2,1)} %get-tuple-element.57.dgate_ref, bf16[384,1024]{1,0:T(8,128)(2,1)} %get-tuple-element.58.dup_ref, f32[384,128]{1,0:T(8,128)} %get-tuple-element.59.score_ref, ...), custom_call_target="tpu_custom_call" | custom-call | flops 4831838208 | bytes 19267584 | tf_op jit(solution)/shard_map/pallas_call | solution.py:314
  348.9 11.7 %shard_map.172 = (bf16[384,1024]{1,0:T(8,128)(2,1)}, bf16[384,1024]{1,0:T(8,128)(2,1)}, bf16[384,1024]{1,0:T(8,128)(2,1)}, f32[384,128]{1,0:T(8,128)}) custom-call(s32[1]{0:T(128)} %bitcast.8.index_ref, bf16[384,2176]{1,0:T(8,128)(2,1)} %collective-permute-done.12.rows_ref, bf16[4,384,2048]{2,1,0:T(8,128)(2,1)} %bitcast.190, ...), custom_call_target="tpu_custom_call" | custom-call | flops 4831838208 | bytes 12582912 | tf_op jit(solution)/shard_map/pallas_call | solution.py:220
  360.6 16.6 %shard_map.173 = bf16[384,4352]{1,0:T(8,128)(2,1)} custom-call(s32[1]{0:T(128)} %bitcast.8.index_ref, bf16[384,1024]{1,0:T(8,128)(2,1)} %get-tuple-element.47.act_ref, bf16[384,1024]{1,0:T(8,128)(2,1)} %get-tuple-element.48.dgate_ref, bf16[384,1024]{1,0:T(8,128)(2,1)} %get-tuple-element.49.dup_ref, f32[384,128]{1,0:T(8,128)} %get-tuple-element.50.score_ref, ...), custom_call_target="tpu_custom_call" | custom-call | flops 4831838208 | bytes 19267584 | tf_op jit(solution)/shard_map/pallas_call | solution.py:314
  387.1 11.7 %shard_map.175 = (bf16[384,1024]{1,0:T(8,128)(2,1)}, bf16[384,1024]{1,0:T(8,128)(2,1)}, bf16[384,1024]{1,0:T(8,128)(2,1)}, f32[384,128]{1,0:T(8,128)}) custom-call(s32[1]{0:T(128)} %bitcast.8.index_ref, bf16[384,2176]{1,0:T(8,128)(2,1)} %constant_dynamic-update-slice_fusion.rows_ref, bf16[4,384,2048]{2,1,0:T(8,128)(2,1)} %bitcast.191, ...), custom_call_target="tpu_custom_call" | custom-call | flops 4831838208 | bytes 12582912 | tf_op jit(solution)/shard_map/pallas_call | solution.py:220
  398.8 17.1 %shard_map.178 = (bf16[96,4352]{1,0:T(8,128)(2,1)}, bf16[96,4352]{1,0:T(8,128)(2,1)}, bf16[96,4352]{1,0:T(8,128)(2,1)}, bf16[96,4352]{1,0:T(8,128)(2,1)}) custom-call(s32[1]{0:T(128)} %bitcast.8.index_ref, bf16[384,1024]{1,0:T(8,128)(2,1)} %get-tuple-element.52.act_ref, bf16[384,1024]{1,0:T(8,128)(2,1)} %get-tuple-element.53.dgate_ref, ...), custom_call_target="tpu_custom_call" | custom-call | flops 4831838208 | bytes 19267584 | tf_op jit(solution)/shard_map/pallas_call | solution.py:314
  416.5 11.9 %shard_map.171 = (bf16[384,1024]{1,0:T(8,128)(2,1)}, bf16[384,1024]{1,0:T(8,128)(2,1)}, bf16[384,1024]{1,0:T(8,128)(2,1)}, f32[384,128]{1,0:T(8,128)}) custom-call(s32[1]{0:T(128)} %bitcast.8.index_ref, bf16[384,2176]{1,0:T(8,128)(2,1)} %pad_maximum_fusion.2.rows_ref, bf16[4,384,2048]{2,1,0:T(8,128)(2,1)} %bitcast.192, ...), custom_call_target="tpu_custom_call" | custom-call | flops 4831838208 | bytes 12582912 | tf_op jit(solution)/shard_map/pallas_call | solution.py:220
  430.5 17.2 %shard_map.174 = (bf16[96,4352]{1,0:T(8,128)(2,1)}, bf16[96,4352]{1,0:T(8,128)(2,1)}, bf16[96,4352]{1,0:T(8,128)(2,1)}, bf16[96,4352]{1,0:T(8,128)(2,1)}) custom-call(s32[1]{0:T(128)} %bitcast.8.index_ref, bf16[384,1024]{1,0:T(8,128)(2,1)} %get-tuple-element.43.act_ref, bf16[384,1024]{1,0:T(8,128)(2,1)} %get-tuple-element.44.dgate_ref, ...), custom_call_target="tpu_custom_call" | custom-call | flops 4831838208 | bytes 19267584 | tf_op jit(solution)/shard_map/pallas_call | solution.py:314
  453.3 16.1 %collective-permute-done.23 = bf16[96,4352]{1,0:T(8,128)(2,1)S(1)} collective-permute-done((bf16[96,4352]{1,0:T(8,128)(2,1)}, bf16[96,4352]{1,0:T(8,128)(2,1)S(1)}, u32[]{:S(2)}, u32[]{:S(2)}) %collective-permute-start.23) | collective-permute-done | bytes 835616 | tf_op jit(solution)/shard_map/ppermute | solution.py:58
  472.1 15.2 %collective-permute-done.21 = bf16[96,4352]{1,0:T(8,128)(2,1)S(1)} collective-permute-done((bf16[96,4352]{1,0:T(8,128)(2,1)}, bf16[96,4352]{1,0:T(8,128)(2,1)S(1)}, u32[]{:S(2)}, u32[]{:S(2)}) %collective-permute-start.21) | collective-permute-done | bytes 835616 | tf_op jit(solution)/shard_map/ppermute | solution.py:58
  493.5 10.5 %collective-permute-done.20 = bf16[96,4352]{1,0:T(8,128)(2,1)S(1)} collective-permute-done((bf16[96,4352]{1,0:T(8,128)(2,1)}, bf16[96,4352]{1,0:T(8,128)(2,1)S(1)}, u32[]{:S(2)}, u32[]{:S(2)}) %collective-permute-start.20) | collective-permute-done | bytes 835616 | tf_op jit(solution)/shard_map/ppermute | solution.py:58
  504.0 5.9 collective-permute-done.24
  509.9 13.7 %collective-permute-done.22 = bf16[96,4352]{1,0:T(8,128)(2,1)S(1)} collective-permute-done((bf16[96,4352]{1,0:T(8,128)(2,1)S(1)}, bf16[96,4352]{1,0:T(8,128)(2,1)S(1)}, u32[]{:S(2)}, u32[]{:S(2)}) %collective-permute-start.22) | collective-permute-done | bytes 835616 | tf_op jit(solution)/shard_map/ppermute | solution.py:63
  562.4 8.5 convolution_convert_fusion
  572.3 6.3 convolution_convert_fusion.2
  583.0 14.0 %collective-permute-done.30 = bf16[192,2048]{1,0:T(8,128)(2,1)S(1)} collective-permute-done((bf16[192,2048]{1,0:T(8,128)(2,1)S(1)}, bf16[192,2048]{1,0:T(8,128)(2,1)S(1)}, u32[]{:S(2)}, u32[]{:S(2)}) %collective-permute-start.30) | collective-permute-done | bytes 786464 | tf_op jit(solution)/shard_map/ppermute | solution.py:58
  601.3 61.2 %all-reduce = (f32[192]{0:T(256)S(1)}, f32[192]{0:T(256)S(1)}) all-reduce(f32[192]{0:T(256)S(1)} %get-tuple-element.105, f32[192]{0:T(256)S(1)} %get-tuple-element.103), channel_id=1, replica_groups=mesh['shard'=4,'ctx'=4,'tp'=2] {'tp'}, use_global_device_ids=true, to_apply=%region_20.21 | all-reduce | flops 384 | bytes 3072 | tf_op jit(solution)/shard_map/psum | solution.py:627
  678.2 6.6 add_bitcast_fusion.1
  688.7 4.6 convolution_convert_fusion.1
  695.4 5.3 shard_map.181
  700.7 5.4 shard_map.179
  706.6 6.4 add_bitcast_fusion.2
  716.7 16.5 %copy.101 = f32[1,2048,2,512]{3,2,1,0:T(2,128)} copy(f32[1,2048,2,512]{3,1,2,0:T(8,128)S(1)} %maximum_bitcast_fusion) | data formatting | bytes 16777216
  735.3 80.7 %all-reduce.4.cloned.1.call-done = f32[20,2048]{1,0:T(8,128)} async-done(((f32[20,2048]{1,0:T(8,128)}), f32[20,2048]{1,0:T(8,128)}) %all-reduce.4.cloned.1.call-update) | async-done | bytes 163856 | tf_op jit(solution)/shard_map/psum | solution.py:673
  818.9 6.8 shard_map.182
  832.5 7.0 shard_map.180
  839.5 6.9 collective-permute-done.40
  849.2 4.3 collective-permute-start.41
  853.5 21.0 %collective-permute-done.38 = bf16[384,1024]{1,0:T(8,128)(2,1)S(1)} collective-permute-done((bf16[384,1024]{1,0:T(8,128)(2,1)}, bf16[384,1024]{1,0:T(8,128)(2,1)S(1)}, u32[]{:S(2)}, u32[]{:S(2)}) %collective-permute-start.38) | collective-permute-done | bytes 786464 | tf_op jit(solution)/shard_map/ppermute | solution.py:58
  880.2 11.1 %collective-permute-done.36 = bf16[384,1024]{1,0:T(8,128)(2,1)S(1)} collective-permute-done((bf16[384,1024]{1,0:T(8,128)(2,1)}, bf16[384,1024]{1,0:T(8,128)(2,1)S(1)}, u32[]{:S(2)}, u32[]{:S(2)}) %collective-permute-start.36) | collective-permute-done | bytes 786464 | tf_op jit(solution)/shard_map/ppermute | solution.py:58
  895.3 8.4 add_bitcast_fusion
  903.7 38.3 %reduce-scatter.2.cloned.1.call-done = bf16[128,1024]{1,0:T(8,128)(2,1)} async-done(((bf16[2048,1024]{1,0:T(8,128)(2,1)}), bf16[128,1024]{1,0:T(8,128)(2,1)}) %reduce-scatter.2.cloned.1.call-update) | async-done | bytes 262160 | tf_op jit(solution)/shard_map/reduce_scatter | solution.py:586
  (474 shorter events, 189.6 us)
Async XLA Ops:
  7.2 106.6 %all-gather.4.cloned.1.call-start = ((), (), s32[]{:S(2)}) async-start(), calls=%async_computation.1 | async-start | bytes 13369344 | tf_op jit(solution)/shard_map/all_gather | solution.py:382
  7.9 162.3 %all-gather.6.cloned.1.call-start = ((), (), s32[]{:S(2)}) async-start(), calls=%async_computation.2 | async-start | bytes 4456448 | tf_op jit(solution)/shard_map/all_gather | solution.py:383
  8.7 255.3 %all-gather.8.cloned.1.call-start = ((), (), s32[]{:S(2)}) async-start(), calls=%async_computation.3 | async-start | bytes 6684672 | tf_op jit(solution)/shard_map/all_gather | solution.py:385
  10.5 805.5 %all-reduce.4.cloned.1.call-start = ((), (), s32[]{:S(2)}) async-start(), calls=%async_computation.5 | async-start | bytes 393216 | tf_op jit(solution)/shard_map/psum | solution.py:673
  129.0 26.2 %collective-permute-start.3 = (bf16[192,1024]{1,0:T(8,128)(2,1)S(1)}, bf16[192,1024]{1,0:T(8,128)(2,1)S(1)}, u32[]{:S(2)}, u32[]{:S(2)}) collective-permute-start(bf16[192,1024]{1,0:T(8,128)(2,1)S(1)} %fusion.55), channel_id=1, source_target_pairs={{0,2},{2,0},{4,6},{6,4},{1,3},{3,1},{5,7},{7,5},{8,10},{10,8},{12,... | collective-permute-start | bytes 1179656 | tf_op jit(solution)/shard_map/ppermute | solution.py:58
  129.0 12.0 %collective-permute-start.4 = (bf16[192,1024]{1,0:T(8,128)(2,1)S(1)}, bf16[192,1024]{1,0:T(8,128)(2,1)S(1)}, u32[]{:S(2)}, u32[]{:S(2)}) collective-permute-start(bf16[192,1024]{1,0:T(8,128)(2,1)S(1)} %fusion.55), channel_id=1, source_target_pairs={{0,4},{2,6},{4,0},{6,2},{1,5},{3,7},{5,1},{7,3},{8,12},{10,14},{12... | collective-permute-start | bytes 1179656 | tf_op jit(solution)/shard_map/ppermute | solution.py:58
  132.7 22.4 %collective-permute-start.1 = (bf16[192,1024]{1,0:T(8,128)(2,1)S(1)}, bf16[192,1024]{1,0:T(8,128)(2,1)S(1)}, u32[]{:S(2)}, u32[]{:S(2)}) collective-permute-start(bf16[192,1024]{1,0:T(8,128)(2,1)S(1)} %fusion.46), channel_id=1, source_target_pairs={{0,4},{2,6},{4,0},{6,2},{1,5},{3,7},{5,1},{7,3},{8,12},{10,14},{12... | collective-permute-start | bytes 1179656 | tf_op jit(solution)/shard_map/ppermute | solution.py:58
  134.5 23.6 %collective-permute-start = (bf16[192,1024]{1,0:T(8,128)(2,1)S(1)}, bf16[192,1024]{1,0:T(8,128)(2,1)S(1)}, u32[]{:S(2)}, u32[]{:S(2)}) collective-permute-start(bf16[192,1024]{1,0:T(8,128)(2,1)S(1)} %fusion.46), channel_id=1, source_target_pairs={{0,2},{2,0},{4,6},{6,4},{1,3},{3,1},{5,7},{7,5},{8,10},{10,8},{12,... | collective-permute-start | bytes 1179656 | tf_op jit(solution)/shard_map/ppermute | solution.py:58
  141.0 14.4 %collective-permute-start.5 = (bf16[192,1024]{1,0:T(8,128)(2,1)S(1)}, bf16[192,1024]{1,0:T(8,128)(2,1)S(1)}, u32[]{:S(2)}, u32[]{:S(2)}) collective-permute-start(bf16[192,1024]{1,0:T(8,128)(2,1)S(1)} %collective-permute-done.4), channel_id=1, source_target_pairs={{0,2},{2,0},{4,6},{6,4},{1,3},{3,1},{5,7},{7,5},{8,10},{10,8},{12,... | collective-permute-start | bytes 1179656 | tf_op jit(solution)/shard_map/ppermute | solution.py:58
  174.3 12.2 %collective-permute-start.6 = (bf16[96,2048]{1,0:T(8,128)(2,1)S(1)}, bf16[96,2048]{1,0:T(8,128)(2,1)}, u32[]{:S(2)}, u32[]{:S(2)}) collective-permute-start(bf16[96,2048]{1,0:T(8,128)(2,1)S(1)} %dynamic-slice_convert_fusion.1), channel_id=1, source_target_pairs={{0,1},{1,0},{2,3},{3,2},{4,5},{5,4},{6,7},{7,6},{8,9},{9,8},{10,11... | collective-permute-start | bytes 1179656 | tf_op jit(solution)/shard_map/ppermute | solution.py:54
  178.6 97.8 %collective-permute-start.10 = (bf16[2048,1024]{1,0:T(8,128)(2,1)}, bf16[2048,1024]{1,0:T(8,128)(2,1)}, u32[]{:S(2)}, u32[]{:S(2)}) collective-permute-start(bf16[2048,1024]{1,0:T(8,128)(2,1)} %pad_maximum_fusion.1.refs_0_.refs_1_), channel_id=1, source_target_pairs={{0,1},{1,0},{2,3},{3,2},{4,5},{5,4},{6,7},{7,6},{8,9},{9,8},{10,11... | collective-permute-start | bytes 12582920 | tf_op jit(solution)/shard_map/ppermute | solution.py:54
  192.6 17.3 %collective-permute-start.7 = (bf16[96,2176]{1,0:T(8,128)(2,1)}, bf16[96,2176]{1,0:T(8,128)(2,1)S(1)}, u32[]{:S(2)}, u32[]{:S(2)}) collective-permute-start(bf16[96,2176]{1,0:T(8,128)(2,1)} %concatenate.99), channel_id=1, source_target_pairs={{0,8},{8,16},{16,24},{24,0},{1,9},{9,17},{17,25},{25,1},{2,10},{10... | collective-permute-start | bytes 1253384 | tf_op jit(solution)/shard_map/ppermute | solution.py:63
  193.1 16.8 %collective-permute-start.14 = (bf16[96,2176]{1,0:T(8,128)(2,1)}, bf16[96,2176]{1,0:T(8,128)(2,1)S(1)}, u32[]{:S(2)}, u32[]{:S(2)}) collective-permute-start(bf16[96,2176]{1,0:T(8,128)(2,1)} %concatenate.99), channel_id=1, source_target_pairs={{0,4},{2,6},{4,0},{6,2},{1,5},{3,7},{5,1},{7,3},{8,12},{10,14},{12... | collective-permute-start | bytes 1253384 | tf_op jit(solution)/shard_map/ppermute | solution.py:58
  193.8 47.5 %collective-permute-start.8 = (bf16[96,2176]{1,0:T(8,128)(2,1)}, bf16[96,2176]{1,0:T(8,128)(2,1)S(1)}, u32[]{:S(2)}, u32[]{:S(2)}) collective-permute-start(bf16[96,2176]{1,0:T(8,128)(2,1)} %concatenate.99), channel_id=1, source_target_pairs={{0,16},{8,24},{16,0},{24,8},{1,17},{9,25},{17,1},{25,9},{2,18},{10... | collective-permute-start | bytes 1253384 | tf_op jit(solution)/shard_map/ppermute | solution.py:63
  195.1 48.5 %collective-permute-start.9 = (bf16[96,2176]{1,0:T(8,128)(2,1)}, bf16[96,2176]{1,0:T(8,128)(2,1)S(1)}, u32[]{:S(2)}, u32[]{:S(2)}) collective-permute-start(bf16[96,2176]{1,0:T(8,128)(2,1)} %concatenate.99), channel_id=1, source_target_pairs={{0,24},{8,0},{16,8},{24,16},{1,25},{9,1},{17,9},{25,17},{2,26},{10... | collective-permute-start | bytes 1253384 | tf_op jit(solution)/shard_map/ppermute | solution.py:63
  209.9 34.2 %collective-permute-start.15 = (bf16[96,2176]{1,0:T(8,128)(2,1)S(1)}, bf16[96,2176]{1,0:T(8,128)(2,1)S(1)}, u32[]{:S(2)}, u32[]{:S(2)}) collective-permute-start(bf16[96,2176]{1,0:T(8,128)(2,1)S(1)} %collective-permute-done.7), channel_id=1, source_target_pairs={{0,4},{2,6},{4,0},{6,2},{1,5},{3,7},{5,1},{7,3},{8,12},{10,14},{12... | collective-permute-start | bytes 1253384 | tf_op jit(solution)/shard_map/ppermute | solution.py:58
  209.9 110.7 %collective-permute-start.11 = (bf16[2048,512]{1,0:T(8,128)(2,1)S(1)}, bf16[2048,512]{1,0:T(8,128)(2,1)}, u32[]{:S(2)}, u32[]{:S(2)}) collective-permute-start(bf16[2048,512]{1,0:T(8,128)(2,1)S(1)} %bitcast.205), channel_id=1, source_target_pairs={{0,1},{1,0},{2,3},{3,2},{4,5},{5,4},{6,7},{7,6},{8,9},{9,8},{10,11... | collective-permute-start | bytes 6291464 | tf_op jit(solution)/shard_map/ppermute | solution.py:54
  241.3 12.5 %collective-permute-start.16 = (bf16[96,2176]{1,0:T(8,128)(2,1)S(1)}, bf16[96,2176]{1,0:T(8,128)(2,1)S(1)}, u32[]{:S(2)}, u32[]{:S(2)}) collective-permute-start(bf16[96,2176]{1,0:T(8,128)(2,1)S(1)} %collective-permute-done.8), channel_id=1, source_target_pairs={{0,4},{2,6},{4,0},{6,2},{1,5},{3,7},{5,1},{7,3},{8,12},{10,14},{12... | collective-permute-start | bytes 1253384 | tf_op jit(solution)/shard_map/ppermute | solution.py:58
  243.6 17.1 %collective-permute-start.17 = (bf16[96,2176]{1,0:T(8,128)(2,1)S(1)}, bf16[96,2176]{1,0:T(8,128)(2,1)S(1)}, u32[]{:S(2)}, u32[]{:S(2)}) collective-permute-start(bf16[96,2176]{1,0:T(8,128)(2,1)S(1)} %collective-permute-done.9), channel_id=1, source_target_pairs={{0,4},{2,6},{4,0},{6,2},{1,5},{3,7},{5,1},{7,3},{8,12},{10,14},{12... | collective-permute-start | bytes 1253384 | tf_op jit(solution)/shard_map/ppermute | solution.py:58
  261.5 59.1 %collective-permute-start.18 = (bf16[384,2176]{1,0:T(8,128)(2,1)}, bf16[384,2176]{1,0:T(8,128)(2,1)}, u32[]{:S(2)}, u32[]{:S(2)}) collective-permute-start(bf16[384,2176]{1,0:T(8,128)(2,1)} %constant_dynamic-update-slice_fusion.rows_ref), channel_id=1, source_target_pairs={{0,2},{2,0},{4,6},{6,4},{1,3},{3,1},{5,7},{7,5},{8,10},{10,8},{12,... | collective-permute-start | bytes 5013512 | tf_op jit(solution)/shard_map/ppermute | solution.py:58
  262.8 86.1 %collective-permute-start.12 = (bf16[384,2176]{1,0:T(8,128)(2,1)}, bf16[384,2176]{1,0:T(8,128)(2,1)}, u32[]{:S(2)}, u32[]{:S(2)}) collective-permute-start(bf16[384,2176]{1,0:T(8,128)(2,1)} %pad_maximum_fusion.2.rows_ref), channel_id=1, source_target_pairs={{0,2},{2,0},{4,6},{6,4},{1,3},{3,1},{5,7},{7,5},{8,10},{10,8},{12,... | collective-permute-start | bytes 5013512 | tf_op jit(solution)/shard_map/ppermute | solution.py:58
  348.9 49.9 %collective-permute-start.19 = (bf16[384,4352]{1,0:T(8,128)(2,1)}, bf16[384,4352]{1,0:T(8,128)(2,1)}, u32[]{:S(2)}, u32[]{:S(2)}) collective-permute-start(bf16[384,4352]{1,0:T(8,128)(2,1)} %shard_map.177), channel_id=1, source_target_pairs={{0,2},{2,0},{4,6},{6,4},{1,3},{3,1},{5,7},{7,5},{8,10},{10,8},{12,... | collective-permute-start | bytes 10027016 | tf_op jit(solution)/shard_map/ppermute | solution.py:58
  377.3 53.2 %collective-permute-start.13 = (bf16[384,4352]{1,0:T(8,128)(2,1)}, bf16[384,4352]{1,0:T(8,128)(2,1)}, u32[]{:S(2)}, u32[]{:S(2)}) collective-permute-start(bf16[384,4352]{1,0:T(8,128)(2,1)} %shard_map.173), channel_id=1, source_target_pairs={{0,2},{2,0},{4,6},{6,4},{1,3},{3,1},{5,7},{7,5},{8,10},{10,8},{12,... | collective-permute-start | bytes 10027016 | tf_op jit(solution)/shard_map/ppermute | solution.py:58
  415.9 35.4 %collective-permute-start.25 = (bf16[96,4352]{1,0:T(8,128)(2,1)}, bf16[96,4352]{1,0:T(8,128)(2,1)S(1)}, u32[]{:S(2)}, u32[]{:S(2)}) collective-permute-start(bf16[96,4352]{1,0:T(8,128)(2,1)} %get-tuple-element.66), channel_id=1, source_target_pairs={{0,4},{2,6},{4,0},{6,2},{1,5},{3,7},{5,1},{7,3},{8,12},{10,14},{12... | collective-permute-start | bytes 2506760 | tf_op jit(solution)/shard_map/ppermute | solution.py:58
  447.6 21.7 %collective-permute-start.23 = (bf16[96,4352]{1,0:T(8,128)(2,1)}, bf16[96,4352]{1,0:T(8,128)(2,1)S(1)}, u32[]{:S(2)}, u32[]{:S(2)}) collective-permute-start(bf16[96,4352]{1,0:T(8,128)(2,1)} %get-tuple-element.64), channel_id=1, source_target_pairs={{0,4},{2,6},{4,0},{6,2},{1,5},{3,7},{5,1},{7,3},{8,12},{10,14},{12... | collective-permute-start | bytes 2506760 | tf_op jit(solution)/shard_map/ppermute | solution.py:58
  449.3 38.0 %collective-permute-start.21 = (bf16[96,4352]{1,0:T(8,128)(2,1)}, bf16[96,4352]{1,0:T(8,128)(2,1)S(1)}, u32[]{:S(2)}, u32[]{:S(2)}) collective-permute-start(bf16[96,4352]{1,0:T(8,128)(2,1)} %get-tuple-element.62), channel_id=1, source_target_pairs={{0,4},{2,6},{4,0},{6,2},{1,5},{3,7},{5,1},{7,3},{8,12},{10,14},{12... | collective-permute-start | bytes 2506760 | tf_op jit(solution)/shard_map/ppermute | solution.py:58
  449.7 54.3 %collective-permute-start.20 = (bf16[96,4352]{1,0:T(8,128)(2,1)}, bf16[96,4352]{1,0:T(8,128)(2,1)S(1)}, u32[]{:S(2)}, u32[]{:S(2)}) collective-permute-start(bf16[96,4352]{1,0:T(8,128)(2,1)} %get-tuple-element.60), channel_id=1, source_target_pairs={{0,4},{2,6},{4,0},{6,2},{1,5},{3,7},{5,1},{7,3},{8,12},{10,14},{12... | collective-permute-start | bytes 2506760 | tf_op jit(solution)/shard_map/ppermute | solution.py:58
  452.7 51.3 %collective-permute-start.26 = (bf16[96,4352]{1,0:T(8,128)(2,1)S(1)}, bf16[96,4352]{1,0:T(8,128)(2,1)S(1)}, u32[]{:S(2)}, u32[]{:S(2)}) collective-permute-start(bf16[96,4352]{1,0:T(8,128)(2,1)S(1)} %add_convert_fusion), channel_id=1, source_target_pairs={{0,8},{8,16},{16,24},{24,0},{1,9},{9,17},{17,25},{25,1},{2,10},{10... | collective-permute-start | bytes 2506760 | tf_op jit(solution)/shard_map/ppermute | solution.py:63
  470.8 39.1 %collective-permute-start.24 = (bf16[96,4352]{1,0:T(8,128)(2,1)S(1)}, bf16[96,4352]{1,0:T(8,128)(2,1)S(1)}, u32[]{:S(2)}, u32[]{:S(2)}) collective-permute-start(bf16[96,4352]{1,0:T(8,128)(2,1)S(1)} %add_convert_fusion.1), channel_id=1, source_target_pairs={{0,16},{8,24},{16,0},{24,8},{1,17},{9,25},{17,1},{25,9},{2,18},{10... | collective-permute-start | bytes 2506760 | tf_op jit(solution)/shard_map/ppermute | solution.py:63
  487.5 36.1 %collective-permute-start.22 = (bf16[96,4352]{1,0:T(8,128)(2,1)S(1)}, bf16[96,4352]{1,0:T(8,128)(2,1)S(1)}, u32[]{:S(2)}, u32[]{:S(2)}) collective-permute-start(bf16[96,4352]{1,0:T(8,128)(2,1)S(1)} %add_convert_fusion.2), channel_id=1, source_target_pairs={{0,24},{8,0},{16,8},{24,16},{1,25},{9,1},{17,9},{25,17},{2,26},{10... | collective-permute-start | bytes 2506760 | tf_op jit(solution)/shard_map/ppermute | solution.py:63
  526.8 10.4 %collective-permute-start.28 = (bf16[96,2048]{1,0:T(8,128)(2,1)S(1)}, bf16[96,2048]{1,0:T(8,128)(2,1)S(1)}, u32[]{:S(2)}, u32[]{:S(2)}) collective-permute-start(bf16[96,2048]{1,0:T(8,128)(2,1)S(1)} %fusion.96), channel_id=1, source_target_pairs={{0,1},{1,0},{2,3},{3,2},{4,5},{5,4},{6,7},{7,6},{8,9},{9,8},{10,11... | collective-permute-start | bytes 1179656 | tf_op jit(solution)/shard_map/ppermute | solution.py:54
  560.6 18.0 %collective-permute-start.29 = (bf16[2,192,2048]{2,1,0:T(8,128)(2,1)S(1)}, bf16[2,192,2048]{2,1,0:T(8,128)(2,1)S(1)}, u32[]{:S(2)}, u32[]{:S(2)}) collective-permute-start(bf16[2,192,2048]{2,1,0:T(8,128)(2,1)S(1)} %pad_maximum_fusion.3), channel_id=1, source_target_pairs={{0,2},{2,0},{4,6},{6,4},{1,3},{3,1},{5,7},{7,5},{8,10},{10,8},{12,... | collective-permute-start | bytes 4718600 | tf_op jit(solution)/shard_map/ppermute | solution.py:58
  570.8 107.4 %collective-permute-start.42 = (bf16[2048,1024]{1,0:T(8,128)(2,1)}, bf16[2048,1024]{1,0:T(8,128)(2,1)}, u32[]{:S(2)}, u32[]{:S(2)}) collective-permute-start(bf16[2048,1024]{1,0:T(8,128)(2,1)} %convolution_convert_fusion), channel_id=1, source_target_pairs={{0,1},{1,0},{2,3},{3,2},{4,5},{5,4},{6,7},{7,6},{8,9},{9,8},{10,11... | collective-permute-start | bytes 12582920 | tf_op jit(solution)/shard_map/ppermute | solution.py:54
  578.9 18.1 %collective-permute-start.30 = (bf16[192,2048]{1,0:T(8,128)(2,1)S(1)}, bf16[192,2048]{1,0:T(8,128)(2,1)S(1)}, u32[]{:S(2)}, u32[]{:S(2)}) collective-permute-start(bf16[192,2048]{1,0:T(8,128)(2,1)S(1)} %fusion.53), channel_id=1, source_target_pairs={{0,4},{2,6},{4,0},{6,2},{1,5},{3,7},{5,1},{7,3},{8,12},{10,14},{12... | collective-permute-start | bytes 2359304 | tf_op jit(solution)/shard_map/ppermute | solution.py:58
  677.7 9.1 collective-permute-start.31
  688.4 253.6 %reduce-scatter.2.cloned.1.call-start = ((), (), s32[]{:S(2)}) async-start(), calls=%async_computation.4 | async-start | bytes 4456448 | tf_op jit(solution)/shard_map/reduce_scatter | solution.py:586
  700.7 118.3 %collective-permute-start.34 = (bf16[4,384,1024]{2,1,0:T(8,128)(2,1)}, bf16[4,384,1024]{2,1,0:T(8,128)(2,1)}, u32[]{:S(2)}, u32[]{:S(2)}) collective-permute-start(bf16[4,384,1024]{2,1,0:T(8,128)(2,1)} %shard_map.181), channel_id=1, source_target_pairs={{0,2},{2,0},{4,6},{6,4},{1,3},{3,1},{5,7},{7,5},{8,10},{10,8},{12,... | collective-permute-start | bytes 9437192 | tf_op jit(solution)/shard_map/ppermute | solution.py:58
  706.1 125.8 %collective-permute-start.33 = (bf16[4,384,1024]{2,1,0:T(8,128)(2,1)}, bf16[4,384,1024]{2,1,0:T(8,128)(2,1)}, u32[]{:S(2)}, u32[]{:S(2)}) collective-permute-start(bf16[4,384,1024]{2,1,0:T(8,128)(2,1)} %shard_map.179), channel_id=1, source_target_pairs={{0,2},{2,0},{4,6},{6,4},{1,3},{3,1},{5,7},{7,5},{8,10},{10,8},{12,... | collective-permute-start | bytes 9437192 | tf_op jit(solution)/shard_map/ppermute | solution.py:58
  714.9 103.0 %collective-permute-start.27 = (bf16[96,2048]{1,0:T(8,128)(2,1)S(1)}, bf16[96,2048]{1,0:T(8,128)(2,1)S(1)}, u32[]{:S(2)}, u32[]{:S(2)}) collective-permute-start(bf16[96,2048]{1,0:T(8,128)(2,1)S(1)} %get-tuple-element.128), channel_id=1, source_target_pairs={{0,1},{1,0},{2,3},{3,2},{4,5},{5,4},{6,7},{7,6},{8,9},{9,8},{10,11... | collective-permute-start | bytes 1179656 | tf_op jit(solution)/shard_map/ppermute | solution.py:54
  733.2 162.1 %collective-permute-start.43 = (bf16[2048,512]{1,0:T(8,128)(2,1)}, bf16[2048,512]{1,0:T(8,128)(2,1)}, u32[]{:S(2)}, u32[]{:S(2)}) collective-permute-start(bf16[2048,512]{1,0:T(8,128)(2,1)} %convolution_convert_fusion.2), channel_id=1, source_target_pairs={{0,1},{1,0},{2,3},{3,2},{4,5},{5,4},{6,7},{7,6},{8,9},{9,8},{10,11... | collective-permute-start | bytes 6291464 | tf_op jit(solution)/shard_map/ppermute | solution.py:54
  734.5 93.3 %collective-permute-start.32 = (f32[96,2048]{1,0:T(8,128)S(1)}, f32[96,2048]{1,0:T(8,128)}, u32[]{:S(2)}, u32[]{:S(2)}) collective-permute-start(f32[96,2048]{1,0:T(8,128)S(1)} %get-tuple-element.127), channel_id=1, source_target_pairs={{0,1},{1,0},{2,3},{3,2},{4,5},{5,4},{6,7},{7,6},{8,9},{9,8},{10,11... | collective-permute-start | bytes 2359304 | tf_op jit(solution)/shard_map/ppermute | solution.py:54
  825.8 20.6 %collective-permute-start.40 = (bf16[384,1024]{1,0:T(8,128)(2,1)}, bf16[384,1024]{1,0:T(8,128)(2,1)S(1)}, u32[]{:S(2)}, u32[]{:S(2)}) collective-permute-start(bf16[384,1024]{1,0:T(8,128)(2,1)} %get-tuple-element.74), channel_id=1, source_target_pairs={{0,4},{2,6},{4,0},{6,2},{1,5},{3,7},{5,1},{7,3},{8,12},{10,14},{12... | collective-permute-start | bytes 2359304 | tf_op jit(solution)/shard_map/ppermute | solution.py:58
  827.2 47.2 %collective-permute-start.38 = (bf16[384,1024]{1,0:T(8,128)(2,1)}, bf16[384,1024]{1,0:T(8,128)(2,1)S(1)}, u32[]{:S(2)}, u32[]{:S(2)}) collective-permute-start(bf16[384,1024]{1,0:T(8,128)(2,1)} %get-tuple-element.72), channel_id=1, source_target_pairs={{0,4},{2,6},{4,0},{6,2},{1,5},{3,7},{5,1},{7,3},{8,12},{10,14},{12... | collective-permute-start | bytes 2359304 | tf_op jit(solution)/shard_map/ppermute | solution.py:58
  829.1 62.2 %collective-permute-start.36 = (bf16[384,1024]{1,0:T(8,128)(2,1)}, bf16[384,1024]{1,0:T(8,128)(2,1)S(1)}, u32[]{:S(2)}, u32[]{:S(2)}) collective-permute-start(bf16[384,1024]{1,0:T(8,128)(2,1)} %get-tuple-element.70), channel_id=1, source_target_pairs={{0,4},{2,6},{4,0},{6,2},{1,5},{3,7},{5,1},{7,3},{8,12},{10,14},{12... | collective-permute-start | bytes 2359304 | tf_op jit(solution)/shard_map/ppermute | solution.py:58
  831.9 111.9 %collective-permute-start.35 = (bf16[384,1024]{1,0:T(8,128)(2,1)}, bf16[384,1024]{1,0:T(8,128)(2,1)}, u32[]{:S(2)}, u32[]{:S(2)}) collective-permute-start(bf16[384,1024]{1,0:T(8,128)(2,1)} %get-tuple-element.68), channel_id=1, source_target_pairs={{0,4},{2,6},{4,0},{6,2},{1,5},{3,7},{5,1},{7,3},{8,12},{10,14},{12... | collective-permute-start | bytes 2359304 | tf_op jit(solution)/shard_map/ppermute | solution.py:58
  849.2 94.7 %collective-permute-start.41 = (bf16[384,1024]{1,0:T(8,128)(2,1)S(1)}, bf16[384,1024]{1,0:T(8,128)(2,1)}, u32[]{:S(2)}, u32[]{:S(2)}) collective-permute-start(bf16[384,1024]{1,0:T(8,128)(2,1)S(1)} %add_convert_fusion.3), channel_id=1, source_target_pairs={{0,24},{8,0},{16,8},{24,16},{1,25},{9,1},{17,9},{25,17},{2,26},{10... | collective-permute-start | bytes 2359304 | tf_op jit(solution)/shard_map/ppermute | solution.py:63
  876.8 67.0 %collective-permute-start.39 = (bf16[384,1024]{1,0:T(8,128)(2,1)}, bf16[384,1024]{1,0:T(8,128)(2,1)}, u32[]{:S(2)}, u32[]{:S(2)}) collective-permute-start(bf16[384,1024]{1,0:T(8,128)(2,1)} %add_convert_fusion.4), channel_id=1, source_target_pairs={{0,16},{8,24},{16,0},{24,8},{1,17},{9,25},{17,1},{25,9},{2,18},{10... | collective-permute-start | bytes 2359304 | tf_op jit(solution)/shard_map/ppermute | solution.py:63
  891.6 52.2 %collective-permute-start.37 = (bf16[384,1024]{1,0:T(8,128)(2,1)S(1)}, bf16[384,1024]{1,0:T(8,128)(2,1)}, u32[]{:S(2)}, u32[]{:S(2)}) collective-permute-start(bf16[384,1024]{1,0:T(8,128)(2,1)S(1)} %add_convert_fusion.5), channel_id=1, source_target_pairs={{0,8},{8,16},{16,24},{24,0},{1,9},{9,17},{17,25},{25,1},{2,10},{10... | collective-permute-start | bytes 2359304 | tf_op jit(solution)/shard_map/ppermute | solution.py:63
  (122 other events, 1894.1 us)
Sparse Core Ops, SparseCore 0:
  10.3 103.4 all-gather.3
  116.0 54.2 all-gather.5
  172.6 79.9 all-gather.7
  688.5 127.4 all-reduce.3
  819.7 122.2 reduce-scatter.1
where the time goes:
time: 962 us; the launch traced here: 954 us
  waiting for transfers between devices  427 us (44%)
  Pallas kernels  151 us (16%)
  local copies, waits for them, and re-layouts  92.7 us (10%)
  blocking collectives  90.8 us (9%)
  matrix products  79.9 us (8%)
  other arithmetic  52.1 us (5%)
  starting transfers between devices  45 us (5%)
  between operations  15.8 us (2%)
    ppermute x26, waiting for transfers between devices, swap_ctx(): lax.ppermute(values_in, 'ctx', [(i, i ^ bit) for i in range(lax.axis_size...  130 us
    psum x1, waiting for transfers between devices, local(): lax.psum(jnp.concatenate([gain_in_grad, gain_mid_grad, qk_gain_part, rout...  80.7 us
    pallas_call x4, Pallas kernels, expert_out(): pl.pallas_call(functools.partial(expert_out_kernel, experts, added is not...  67.5 us
    ppermute x9, waiting for transfers between devices, shift_shard(): lax.ppermute(values_in, 'shard', [(i, (i + step) % size) for i in range(s...  61.9 us
    psum x1, blocking collectives, local(): lax.psum((jnp.sum(q_scaled * q_hat, axis=1), jnp.sum(k_scaled * k_hat, ax...  61.2 us
    all_gather x1, waiting for transfers between devices, local(): qkv_all = lax.all_gather(w_qkv, owners, axis=0, tiled=True)  55.7 us
    ppermute x9, waiting for transfers between devices, swap_tp(): return lax.ppermute(values_in, 'tp', [(0, 1), (1, 0)])  50.7 us
    pallas_call x4, Pallas kernels, expert_in(): pl.pallas_call(functools.partial(expert_in_kernel, experts), out_shape=[j...  47 us
  transfers between devices with their start and end apart: 49, of which 23 were waited for; matrix products, arithmetic and copies ran while one was open for 19% of the time, Pallas kernels for 16%

commit v1 on v0

--- a/solution.py
+++ b/solution.py
@@ -11,6 +11,8 @@
 
 HEAD = 128
 LANES = 128
+SHARD, CTX, TP = "shard", "ctx", "tp"
+OWNERS = (SHARD, CTX)
 
 
 norm_eps = 1e-05
@@ -51,16 +53,16 @@
 
 
 def swap_tp(values_in):
-    return lax.ppermute(values_in, "tp", [(0, 1), (1, 0)])
+    return lax.ppermute(values_in, TP, [(0, 1), (1, 0)])
 
 
 def swap_ctx(values_in, bit):
-    return lax.ppermute(values_in, "ctx", [(i, i ^ bit) for i in range(lax.axis_size("ctx"))])
+    return lax.ppermute(values_in, CTX, [(i, i ^ bit) for i in range(lax.axis_size(CTX))])
 
 
 def shift_shard(values_in, step):
-    size = lax.axis_size("shard")
-    return lax.ppermute(values_in, "shard", [(i, (i + step) % size) for i in range(size)])
+    size = lax.axis_size(SHARD)
+    return lax.ppermute(values_in, SHARD, [(i, (i + step) % size) for i in range(size)])
 
 
 def row_major(values_in):
@@ -134,79 +136,55 @@
     )(order, *operands)
 
 
-def reorder_kernel(order_ref, rows_ref, out_ref):
-    out_ref[...] = rows_ref[...]
-
-
-def reorder_blocks(order, rows):
-    spec = (1,) + rows.shape[1:]
-    return pl.pallas_call(
-        reorder_kernel,
-        out_shape=jax.ShapeDtypeStruct(rows.shape, rows.dtype),
-        grid_spec=pltpu.PrefetchScalarGridSpec(
-            num_scalar_prefetch=1,
-            grid=(rows.shape[0],),
-            in_specs=[pl.BlockSpec(spec, lambda i, order: (order[i], 0, 0))],
-            out_specs=pl.BlockSpec(spec, lambda i, order: (i, 0, 0)),
-        ),
-        cost_estimate=pl.CostEstimate(
-            flops=0, bytes_accessed=2 * rows.size * rows.dtype.itemsize, transcendentals=0
-        ),
-    )(order, rows)
-
-
 TILE = 256
 
 
-def expert_in_kernel(experts, index_ref, rows_ref, grads_ref, *refs):
+def expert_in_kernel(experts, index_ref, *refs):
     f32, bf16 = jnp.float32, jnp.bfloat16
-    weights, (act_ref, dgate_ref, dup_ref, score_ref) = refs[:6], refs[6:]
-    width = weights[0].shape[0]
+    rows_refs, grads_refs, weights = refs[:2], refs[2:4], refs[4:10]
+    act_ref, dgate_ref, dup_ref, score_ref = refs[10:]
+    width, count = weights[0].shape[0], rows_refs[0].shape[0]
     tile = pl.program_id(0)
 
     def through(gate_ref, up_ref, back_ref):
-        extra = rows_ref[:, width:].astype(f32)
-        column = lax.broadcasted_iota(jnp.int32, extra.shape, 1)
-        mine_in = (column % experts == index_ref[0]) & (column < 3 * experts)
-        gate_col = jnp.sum(jnp.where(mine_in, extra, 0.0), axis=1, keepdims=True)
-        rows = rows_ref[:, :width]
-        gate_val = jnp.dot(rows, gate_ref[...], preferred_element_type=f32)
-        up_val = jnp.dot(rows, up_ref[...], preferred_element_type=f32)
-        hidden_raw = jnp.dot(grads_ref[0], back_ref[...], preferred_element_type=f32)
-        gate_sig = jax.nn.sigmoid(gate_val)
-        gate_act = gate_val * gate_sig
-        hidden_act = gate_act * up_val
-        act_ref[...] = (gate_col * hidden_act).astype(bf16)
-        hidden_grad = gate_col * hidden_raw
-        dgate = hidden_grad * up_val * gate_sig * (1.0 + gate_val * (1.0 - gate_sig))
-        dgate_ref[...] = dgate.astype(bf16)
-        dup_ref[...] = (hidden_grad * gate_act).astype(bf16)
-        score = hidden_act * hidden_raw
-        lanes = score[:, :LANES]
-        for start in range(LANES, TILE, LANES):
-            lanes = lanes + score[:, start : start + LANES]
-
-        @pl.when(tile == 0)
-        def _():
-            score_ref[...] = lanes
-
-        @pl.when(tile > 0)
-        def _():
-            score_ref[...] += lanes
-
-    side = pl.num_programs(0) // 2
-
-    @pl.when(tile < side)
+        for side in range(2):
+            here = slice(side * count, (side + 1) * count)
+            extra = rows_refs[side][:, width:].astype(f32)
+            column = lax.broadcasted_iota(jnp.int32, extra.shape, 1)
+            mine_in = (column % experts == index_ref[0]) & (column < 3 * experts)
+            gate_col = jnp.sum(jnp.where(mine_in, extra, 0.0), axis=1, keepdims=True)
+            rows = rows_refs[side][:, :width]
+            gate_val = jnp.dot(rows, gate_ref[...], preferred_element_type=f32)
+            up_val = jnp.dot(rows, up_ref[...], preferred_element_type=f32)
+            hidden_raw = jnp.dot(grads_refs[side][...], back_ref[...], preferred_element_type=f32)
+            gate_sig = jax.nn.sigmoid(gate_val)
+            gate_act = gate_val * gate_sig
+            hidden_act = gate_act * up_val
+            act_ref[here, :] = (gate_col * hidden_act).astype(bf16)
+            hidden_grad = gate_col * hidden_raw
+            dgate = hidden_grad * up_val * gate_sig * (1.0 + gate_val * (1.0 - gate_sig))
+            dgate_ref[here, :] = dgate.astype(bf16)
+            dup_ref[here, :] = (hidden_grad * gate_act).astype(bf16)
+            score = hidden_act * hidden_raw
+            lanes = score[:, :LANES]
+            for start in range(LANES, TILE, LANES):
+                lanes = lanes + score[:, start : start + LANES]
+            before = jnp.where(tile == 0, 0.0, score_ref[here, :])
+            score_ref[here, :] = before + lanes
+
+    side_tiles = pl.num_programs(0) // 2
+
+    @pl.when(tile < side_tiles)
     def _():
         through(*weights[:3])
 
-    @pl.when(tile >= side)
+    @pl.when(tile >= side_tiles)
     def _():
         through(*weights[3:])
 
 
-def expert_in(index, rows, grads, group, own, other, experts):
-    count, columns = rows.shape
+def expert_in(index, rows, grads, own, other, experts):
+    count, columns = rows[0].shape
     width, hidden = own[1].shape
     side = hidden // TILE
 
@@ -216,30 +194,32 @@
         )
 
     weight_specs = [tiles(shift, base) for shift in (0, side) for base in (0, side, 0)]
-    wide = pl.BlockSpec((count, TILE), lambda h, index: (0, h))
+    wide = pl.BlockSpec((2 * count, TILE), lambda h, index: (0, h))
     return pl.pallas_call(
         functools.partial(expert_in_kernel, experts),
-        out_shape=[jax.ShapeDtypeStruct((count, 2 * hidden), jnp.bfloat16)] * 3
-        + [jax.ShapeDtypeStruct((count, LANES), jnp.float32)],
+        out_shape=[jax.ShapeDtypeStruct((2 * count, 2 * hidden), jnp.bfloat16)] * 3
+        + [jax.ShapeDtypeStruct((2 * count, LANES), jnp.float32)],
         grid_spec=pltpu.PrefetchScalarGridSpec(
             num_scalar_prefetch=1,
             grid=(2 * side,),
-            in_specs=[
-                pl.BlockSpec((count, columns), lambda h, index: (0, 0)),
-                pl.BlockSpec((1, count, width), lambda h, index: (group, 0, 0)),
-            ]
-            + weight_specs,
-            out_specs=[wide, wide, wide, pl.BlockSpec((count, LANES), lambda h, index: (0, 0))],
+            in_specs=[fixed((count, columns))] * 2 + [fixed((count, width))] * 2 + weight_specs,
+            out_specs=[wide, wide, wide, fixed((2 * count, LANES))],
         ),
         cost_estimate=pl.CostEstimate(
-            flops=12 * count * width * hidden,
+            flops=24 * count * width * hidden,
             bytes_accessed=12 * width * hidden,
-            transcendentals=2 * count * hidden,
+            transcendentals=4 * count * hidden,
         ),
-    )(index, rows, grads, own[0], own[0], own[1], other[0], other[0], other[1])
-
-
-def expert_out_kernel(experts, added, index_ref, act_ref, dgate_ref, dup_ref, score_ref, *refs):
+    )(index, *rows, *grads, own[0], own[0], own[1], other[0], other[0], other[1])
+
+
+def fixed(shape):
+    return pl.BlockSpec(
+        shape, lambda h, index: (0,) * len(shape), pipeline_mode=pl.Buffered(1)
+    )
+
+
+def expert_out_kernel(added, act_ref, dgate_ref, dup_ref, *refs):
     f32, bf16 = jnp.float32, jnp.bfloat16
     down_own, pair_own, down_other, pair_other = refs[:4]
     outs = refs[5:] if added else refs[4:]
@@ -267,7 +247,7 @@
             + times(act_ref[:, hidden:], down_other[...])
         )
 
-    @pl.when((step >= side) & (step < 2 * side))
+    @pl.when(step >= side)
     def _():
         put(
             times(dgate_ref[:, :hidden], pair_own[:, :hidden])
@@ -276,56 +256,34 @@
             + times(dup_ref[:, hidden:], pair_other[:, hidden:])
         )
 
-    @pl.when(step == 2 * side)
-    def _():
-        score = jnp.sum(score_ref[...], axis=1, keepdims=True)
-        high = score.astype(bf16).astype(f32)
-        spot = lax.broadcasted_iota(jnp.int32, (score.shape[0], TILE), 1)
-        rest = jnp.where(spot == index_ref[0] + experts, score - high, 0.0)
-        put(jnp.where(spot == index_ref[0], high, rest))
-
-
-def expert_out(index, act, dgate, dup, score, own, other, experts, pieces, added=None):
-    count = act.shape[0]
+
+def expert_out(half_of, act, dgate, dup, own, other, pieces, added=None):
+    count = act.shape[0] // 2
     width, hidden = own[1].shape
-    side = width // TILE
-    total = (2 * side + 1) * TILE
-    whole = pl.BlockSpec((count, 2 * hidden), lambda n, index: (0, 0))
-    wide = pl.BlockSpec((count, TILE), lambda n, index: (0, n))
-    down_spec = pl.BlockSpec((TILE, hidden), lambda n, index: (jnp.minimum(n, side - 1), 0))
-    pair_spec = pl.BlockSpec(
-        (TILE, 2 * hidden), lambda n, index: (jnp.clip(n - side, 0, side - 1), 0)
-    )
-    in_specs = [
-        whole,
-        whole,
-        whole,
-        pl.BlockSpec((count, LANES), lambda n, index: (0, 0)),
-        down_spec,
-        pair_spec,
-        down_spec,
-        pair_spec,
-    ]
-    operands = [act, dgate, dup, score, own[1], own[0], other[1], other[0]]
+    tile = 2 * TILE
+    side = width // tile
+    whole = pl.BlockSpec((count, 2 * hidden), lambda n: (half_of, 0))
+    wide = pl.BlockSpec((count, tile), lambda n: (0, n))
+    down_spec = pl.BlockSpec((tile, hidden), lambda n: (jnp.minimum(n, side - 1), 0))
+    pair_spec = pl.BlockSpec((tile, 2 * hidden), lambda n: (jnp.clip(n - side, 0, side - 1), 0))
+    in_specs = [whole] * 3 + [down_spec, pair_spec] * 2
+    operands = [act, dgate, dup, own[1], own[0], other[1], other[0]]
     if added is not None:
         in_specs.append(wide)
         operands.append(added)
     rows = count // pieces
     return pl.pallas_call(
-        functools.partial(expert_out_kernel, experts, added is not None),
-        out_shape=[jax.ShapeDtypeStruct((rows, total), jnp.bfloat16)] * pieces,
-        grid_spec=pltpu.PrefetchScalarGridSpec(
-            num_scalar_prefetch=1,
-            grid=(2 * side + 1,),
-            in_specs=in_specs,
-            out_specs=[pl.BlockSpec((rows, TILE), lambda n, index: (0, n))] * pieces,
-        ),
+        functools.partial(expert_out_kernel, added is not None),
+        out_shape=[jax.ShapeDtypeStruct((rows, 2 * width), jnp.bfloat16)] * pieces,
+        grid=(2 * side,),
+        in_specs=in_specs,
+        out_specs=[pl.BlockSpec((rows, tile), lambda n: (0, n))] * pieces,
         cost_estimate=pl.CostEstimate(
             flops=12 * count * width * hidden,
-            bytes_accessed=12 * width * hidden + 4 * count * total,
+            bytes_accessed=12 * width * hidden + 8 * count * width,
             transcendentals=0,
         ),
-    )(index, *operands)
+    )(*operands)
 
 
 def join_halves(mine, other, first_is_mine):
@@ -361,11 +319,11 @@
     experts = router.shape[1]
     hidden = w_down.shape[2]
     half = tokens // 2
-    owners = ("shard", "ctx")
-    tp_index = lax.axis_index("tp")
-    ctx_index = lax.axis_index("ctx")
-    ctx_size = lax.axis_size("ctx")
-    expert_index = lax.axis_index("shard") * ctx_size + ctx_index
+    owners = OWNERS
+    tp_index = lax.axis_index(TP)
+    ctx_index = lax.axis_index(CTX)
+    ctx_size = lax.axis_size(CTX)
+    expert_index = lax.axis_index(SHARD) * ctx_size + ctx_index
     first_is_mine = tp_index == 0
     my_row = tp_index * half
     other_row = (1 - tp_index) * half
@@ -382,7 +340,21 @@
     qkv_all = lax.all_gather(w_qkv, owners, axis=0, tiled=True)
     out_all = lax.all_gather(w_out, owners, axis=0, tiled=True)
     grad_half = my_rows(out_grad)
-    grad_rows = lax.all_gather(grad_half, owners, axis=0, tiled=True)
+    shards = lax.axis_size(SHARD)
+    shard_index = lax.axis_index(SHARD)
+    steps = range(shards)
+
+    def gather_groups(block):
+        near_blocks = [block] + [shift_shard(block, step) for step in steps[1:]]
+        far_blocks = [swap_ctx(block, 2) for block in near_blocks]
+        near_group = row_major(jnp.concatenate(near_blocks, axis=0))
+        far_group = row_major(jnp.concatenate(far_blocks, axis=0))
+        return [
+            [near_group, swap_ctx(near_group, 1)],
+            [far_group, swap_ctx(far_group, 1)],
+        ]
+
+    grad_groups = gather_groups(grad_half)
     pair_own = jnp.concatenate([w_gate_up[0, :, 0], w_gate_up[0, :, 1]], axis=1)
     pair_other = swap_tp(pair_own)
 
@@ -390,7 +362,7 @@
         return which[:, index * hidden : (index + 1) * hidden]
 
     half_width = qkv_all.shape[1]
-    full_heads = half_width * lax.axis_size("tp")
+    full_heads = half_width * lax.axis_size(TP)
     head_count = half_width // HEAD
     gains_f = small_all[:, :4].astype(f32)
     router_f = small_all[:, 4:].astype(f32)
@@ -421,7 +393,7 @@
     )
     v_low = v_raw.astype(bf16)
     square_q, square_k = lax.psum(
-        (jnp.sum(q_raw * q_raw, axis=1), jnp.sum(k_raw * k_raw, axis=1)), "tp"
+        (jnp.sum(q_raw * q_raw, axis=1), jnp.sum(k_raw * k_raw, axis=1)), TP
     )
     down_own = lax.optimization_barrier((w_down[0], square_q))[0]
     down_other = swap_tp(down_own)
@@ -479,54 +451,24 @@
             parts = parts + [jnp.zeros((parts[0].shape[0], rest), parts[0].dtype)]
         return jnp.concatenate(parts, axis=1)
 
-    shards = lax.axis_size("shard")
-    shard_index = lax.axis_index("shard")
-    steps = range(shards)
-
-    def block_of(step, far, side):
-        return ((shard_index + shards - step) % shards) * ctx_size + (
-            ctx_index ^ (2 * far + side)
-        )
-
-    mid_block = row_major(padded([mid_norm.astype(bf16)] + split_three(gates)))
-    near_blocks = [mid_block] + [shift_shard(mid_block, step) for step in steps[1:]]
-    far_blocks = [swap_ctx(block, 2) for block in near_blocks]
-    near_group = row_major(jnp.concatenate(near_blocks, axis=0))
-    far_group = row_major(jnp.concatenate(far_blocks, axis=0))
-    mid_groups = [
-        [near_group, swap_ctx(near_group, 1)],
-        [far_group, swap_ctx(far_group, 1)],
+    mid_groups = gather_groups(row_major(padded([mid_norm.astype(bf16)] + split_three(gates))))
+    index = expert_index.astype(jnp.int32).reshape(1)
+    inside = [
+        expert_in(index, mid_groups[far], grad_groups[far], own_weights, other_weights, experts)
+        for far in range(2)
     ]
-    turn_order = jnp.stack(
-        [block_of(step, far, side) for far in range(2) for side in range(2) for step in steps]
-    ).astype(jnp.int32)
-    grad_groups = reorder_blocks(turn_order, grad_rows.reshape(-1, half, width)).reshape(
-        4, shards * half, width
-    )
-    index = expert_index.astype(jnp.int32).reshape(1)
-    inside = {
-        (far, side): expert_in(
-            index, mid_groups[far][side], grad_groups, 2 * far + side, own_weights, other_weights, experts
-        )
-        for far in range(2)
-        for side in range(2)
-    }
-
-    def sum_side(far):
-        sent = expert_out(index, *inside[far, 1], own_weights, other_weights, experts, 1)[0]
-        return expert_out(
-            index,
-            *inside[far, 0],
-            own_weights,
-            other_weights,
-            experts,
-            shards,
-            swap_ctx(sent, 1),
-        )
-
-    far_sums = sum_side(1)
+
+    def send_side(far):
+        sent = expert_out(1, *inside[far][:3], own_weights, other_weights, 1)[0]
+        return swap_ctx(sent, 1)
+
+    def sum_side(far, arrived):
+        return expert_out(0, *inside[far][:3], own_weights, other_weights, shards, arrived)
+
+    arrived_sides = [send_side(1), send_side(0)]
+    far_sums = sum_side(1, arrived_sides[0])
     far_arrived = [swap_ctx(far_sums[step], 2) for step in steps]
-    near_sums = sum_side(0)
+    near_sums = sum_side(0, arrived_sides[1])
     block_sums = [add_low(mine, other) for mine, other in zip(near_sums, far_arrived)]
     step_arrived = [
         shift_shard(block_sums[step].astype(bf16), -step) for step in steps[1:]
@@ -534,11 +476,11 @@
     block_total = row_major(add_low(block_sums[0], *step_arrived))
 
     pairs = [(far, side) for far in range(2) for side in range(2)]
-    mid_all = jnp.concatenate([mid_groups[far][side][:, :width] for far, side in pairs], axis=0)
+    mid_all = jnp.concatenate([mid_groups[far][side] for far, side in pairs], axis=0)[:, :width]
     act_all, dgate_all, dup_all = (
-        jnp.concatenate([inside[pair][which] for pair in pairs], axis=0) for which in range(3)
-    )
-    grad_all = grad_groups.reshape(-1, width)
+        jnp.concatenate([inside[far][which] for far in range(2)], axis=0) for which in range(3)
+    )
+    grad_all = jnp.concatenate([grad_groups[far][side] for far, side in pairs], axis=0)
 
     def over_tokens(rows, columns):
         return lax.dot_general(
@@ -560,12 +502,21 @@
     )[None]
     down_sent = over_tokens(grad_all, hidden_part(act_all, 1)).astype(bf16)
 
+    score_rel = jnp.concatenate([jnp.sum(inside[far][3], axis=1) for far in range(2)], axis=0)
+    blocks = jnp.arange(shards * ctx_size, dtype=jnp.int32)
+    place = (ctx_index ^ (blocks % ctx_size)) * shards + (
+        shard_index + shards - blocks // ctx_size
+    ) % shards
+    score_abs = jnp.take(score_rel.reshape(-1, half), place, axis=0)
+    score_total = lax.all_to_all(
+        score_abs, owners, split_axis=0, concat_axis=0, tiled=True
+    ).T
+
     mixture = block_total[:, :width]
     mid_grad = block_total[:, width : 2 * width]
-    scores_in = block_total[:, 2 * width :]
-    score_total = scores_in[:, :experts] + scores_in[:, experts : 2 * experts]
     output_half = (resid + mixture).astype(bf16)
-    output = join_halves(output_half, swap_tp(output_half), first_is_mine)
+    output_other = swap_tp(output_half)
+    output = join_halves(output_half, output_other, first_is_mine)
     logit_grad = gates * (score_total - jnp.sum(gates * score_total, axis=1, keepdims=True))
     router_grad = lax.dot_general(
         logit_grad, mid_norm, (((0,), (0,)), ((), ())), precision=highest
@@ -625,7 +576,7 @@
     q_scaled = gain_q * q_in
     k_scaled = gain_k * k_in
     inner_q, inner_k = lax.psum(
-        (jnp.sum(q_scaled * q_hat, axis=1), jnp.sum(k_scaled * k_hat, axis=1)), "tp"
+        (jnp.sum(q_scaled * q_hat, axis=1), jnp.sum(k_scaled * k_hat, axis=1)), TP
     )
     down_sent = lax.optimization_barrier((down_sent, inner_q))[0]
     down_arrived = swap_tp(down_sent)
@@ -669,21 +620,28 @@
     qk_gain_part = lax.dynamic_update_slice(
         jnp.zeros((2, width), f32), gain_pair, (0, tp_index * half_width)
     )
-    everyone = ("shard", "ctx", "tp")
-    small_total = lax.psum(
-        jnp.concatenate([gain_in_grad, gain_mid_grad, qk_gain_part, router_grad], axis=0),
-        everyone,
-    )
-    small_owned = lax.dynamic_slice_in_dim(
-        small_total, expert_index * norm_gains.shape[0], norm_gains.shape[0], axis=1
-    ).T
+    early_total = lax.psum(jnp.concatenate([router_grad, gain_mid_grad], axis=0), (SHARD, CTX, TP))
+    late = jnp.concatenate([gain_in_grad, qk_gain_part], axis=0)
+    late = late + swap_tp(late)
+    late = late + swap_ctx(late, 1)
+    late = late + swap_ctx(late, 2)
+    late_total = late + sum(shift_shard(late, step) for step in steps[1:])
+
+    def owned(total):
+        count = norm_gains.shape[0]
+        return lax.dynamic_slice_in_dim(total, expert_index * count, count, axis=1)
+
+    gains_total = jnp.concatenate([late_total[:1], early_total[experts:], late_total[1:]], axis=0)
+    gains_owned = owned(gains_total).T
+    router_owned = owned(early_total[:experts]).T
+
     return (
         output,
         input_grad,
         qkv_owned,
         out_owned,
-        small_owned[:, :4],
-        small_owned[:, 4:],
+        gains_owned,
+        router_owned,
         gate_up_grad,
         down_grad,
     )
@@ -691,27 +649,27 @@
 
 def solution(mesh):
     in_specs = (
-        P(("shard", "ctx"), None),
-        P(("shard", "ctx"), "tp"),
-        P(("shard", "ctx"), "tp"),
-        P(("shard", "ctx"), None),
-        P(("shard", "ctx"), None),
-        P(("shard", "ctx"), None, None, "tp"),
-        P(("shard", "ctx"), None, "tp"),
-        P(("shard", "ctx"), None),
-        P("shard", None),
-        P("shard", None),
-        P(("shard", "ctx"), None),
+        P(OWNERS, None),
+        P(OWNERS, TP),
+        P(OWNERS, TP),
+        P(OWNERS, None),
+        P(OWNERS, None),
+        P(OWNERS, None, None, TP),
+        P(OWNERS, None, TP),
+        P(OWNERS, None),
+        P(SHARD, None),
+        P(SHARD, None),
+        P(OWNERS, None),
     )
     out_specs = (
-        P(("shard", "ctx"), None),
-        P(("shard", "ctx"), None),
-        P(("shard", "ctx"), "tp"),
-        P(("shard", "ctx"), "tp"),
-        P(("shard", "ctx"), None),
-        P(("shard", "ctx"), None),
-        P(("shard", "ctx"), None, None, "tp"),
-        P(("shard", "ctx"), None, "tp"),
+        P(OWNERS, None),
+        P(OWNERS, None),
+        P(OWNERS, TP),
+        P(OWNERS, TP),
+        P(OWNERS, None),
+        P(OWNERS, None),
+        P(OWNERS, None, None, TP),
+        P(OWNERS, None, TP),
     )
 
     return jax.shard_map(local, mesh=mesh, in_specs=in_specs, out_specs=out_specs, check_vma=False)

time: 962 us -> 981 us (1.020)
  blocking collectives: 90.8 us -> 48.4 us
  Pallas kernels: 151 us -> 110 us
  waiting for transfers between devices: 427 us -> 468 us
  starting transfers between devices: 45 us -> 77.8 us
  other arithmetic: 52.1 us -> 74 us
    psum x1, blocking collectives: 61.2 us -> 5.12 us  [local(): lax.psum((jnp.sum(q_scaled * q_hat, axis=1), jnp.sum(k_scaled * k_hat, ax...]
    ppermute x44 -> x59, waiting for transfers between devices: 243 us -> 295 us  [the longest x10 130 us: swap_tp(): return lax.ppermute(values_in, TP, [(0, 1), (1, 0)])]
    reduce_scatter x1, waiting for transfers between devices: 38.3 us -> 0.01 us  [local(): lax.psum_scatter(out_proj_grad, owners, scatter_dimension=0, tiled=True)]
    pallas_call x5 -> x4, Pallas kernels: 79.1 us -> 50.3 us  [expert_out(): pl.pallas_call(functools.partial(expert_out_kernel, added is not None), o...]
    psum x1, waiting for transfers between devices: 80.7 us -> 107 us  [local(): lax.psum(jnp.concatenate([router_grad, gain_mid_grad], axis=0), (SHARD, C...]
    ppermute x44 -> x59, starting transfers between devices: 44.6 us -> 70.1 us  [the longest x15 34.2 us: shift_shard(): lax.ppermute(values_in, SHARD, [(i, (i + step) % size) for i in range(siz...]
    all_gather x1, blocking collectives: 24.2 us -> 37.8 us  [local(): lax.all_gather(jnp.concatenate([norm_gains, router], axis=1), owners, axi...]
    slice x6 -> x5, local copies, waits for them, and re-layouts: 13.4 us -> 1.06 us  [the longest x1 1.03 us: local(): router_owned = owned(early_total[:experts]).T]
  transfers between devices with their start and end apart: 49 -> 64, of which waited for: 23 -> 28; matrix products, arithmetic and copies ran while one was open for 19% -> 19% of each run, Pallas kernels for 16% -> 11%
where the time goes in v1:
time: 981 us; the launch traced here: 974 us
  waiting for transfers between devices  468 us (48%)
  Pallas kernels  110 us (11%)
  local copies, waits for them, and re-layouts  91.8 us (9%)
  matrix products  88 us (9%)
  starting transfers between devices  77.8 us (8%)
  other arithmetic  74 us (8%)
  blocking collectives  48.4 us (5%)
  between operations  15.7 us (2%)
    ppermute x10, waiting for transfers between devices, swap_tp(): return lax.ppermute(values_in, TP, [(0, 1), (1, 0)])  130 us
    ppermute x34, waiting for transfers between devices, swap_ctx(): lax.ppermute(values_in, CTX, [(i, i ^ bit) for i in range(lax.axis_size(C...  109 us
    psum x1, waiting for transfers between devices, local(): lax.psum(jnp.concatenate([router_grad, gain_mid_grad], axis=0), (SHARD, C...  107 us
    ppermute x15, waiting for transfers between devices, shift_shard(): lax.ppermute(values_in, SHARD, [(i, (i + step) % size) for i in range(siz...  56 us
    all_gather x1, waiting for transfers between devices, local(): qkv_all = lax.all_gather(w_qkv, owners, axis=0, tiled=True)  54.8 us
    pallas_call x4, Pallas kernels, expert_out(): pl.pallas_call(functools.partial(expert_out_kernel, added is not None), o...  50.3 us
    dot_general x5, matrix products, over_tokens(): lax.dot_general(rows, columns, (((0,), (0,)), ((), ())), preferred_elemen...  44.4 us
    unnamed x246, local copies, waits for them, and re-layouts  43 us
  transfers between devices with their start and end apart: 64, of which 28 were waited for; matrix products, arithmetic and copies ran while one was open for 19% of the time, Pallas kernels for 11%

profile of v1, /device:TPU:0, one launch (start us, length us, event | category | flops | bytes accessed | tf_op | source)
XLA Modules:
  0.0 973.6 jit_solution(11225300997907106451)
XLA Ops:
  19.7 37.8 %all_gather.9 = bf16[2048,20]{0,1:T(8,128)(2,1)S(1)} all-gather(bf16[128,20]{0,1:T(8,128)(2,1)S(1)} %pad_maximum_fusion.22), channel_id=1, replica_groups=mesh['shard'=4,'ctx'=4,'tp'=2] {'shard','ctx'}, dimensions={0}, use_global_device_ids=true | all-gather | bytes 87040 | tf_op jit(solution)/shard_map/all_gather | solution.py:337
  63.1 9.1 fusion.119
  75.5 54.8 %all-gather.3.cloned.1.call-done = bf16[6144,1024]{1,0:T(8,128)(2,1)} async-done(((bf16[384,1024]{1,0:T(8,128)(2,1)}), bf16[6144,1024]{1,0:T(8,128)(2,1)}) %all-gather.3.cloned.1.call-update) | async-done | bytes 12582928 | tf_op jit(solution)/shard_map/all_gather | solution.py:340
  137.2 5.5 all-reduce.1
  151.3 6.5 collective-permute-done.4
  158.0 13.8 %collective-permute-done.1 = bf16[192,1024]{1,0:T(8,128)(2,1)S(1)} collective-permute-done((bf16[192,1024]{1,0:T(8,128)(2,1)S(1)}, bf16[192,1024]{1,0:T(8,128)(2,1)S(1)}, u32[]{:S(2)}, u32[]{:S(2)}) %collective-permute-start.1) | collective-permute-done | bytes 393248 | tf_op jit(solution)/shard_map/ppermute | solution.py:60
  179.1 9.9 %all-gather.5.cloned.1.call-done = bf16[2048,1024]{1,0:T(8,128)(2,1)} async-done(((bf16[128,1024]{1,0:T(8,128)(2,1)}), bf16[2048,1024]{1,0:T(8,128)(2,1)}) %all-gather.5.cloned.1.call-update) | async-done | bytes 4194320 | tf_op jit(solution)/shard_map/all_gather | solution.py:341
  189.0 3.8 fusion.70
  195.7 4.4 pad_maximum_fusion.7.refs_4_.refs_5_.refs_1_
  201.3 4.8 collective-permute-done.6
  212.5 4.0 collective-permute-start.7
  232.8 11.9 %collective-permute-done.8 = bf16[96,2176]{1,0:T(8,128)(2,1)S(1)} collective-permute-done((bf16[96,2176]{1,0:T(8,128)(2,1)}, bf16[96,2176]{1,0:T(8,128)(2,1)S(1)}, u32[]{:S(2)}, u32[]{:S(2)}) %collective-permute-start.8) | collective-permute-done | bytes 417824 | tf_op jit(solution)/shard_map/ppermute | solution.py:65
  250.0 7.2 collective-permute-done.20
  258.0 7.1 collective-permute-done.21
  272.2 23.9 %collective-permute-done.15.refs_7_.refs_8_.refs_3_ = bf16[2048,1024]{1,0:T(8,128)(2,1)} collective-permute-done((bf16[2048,1024]{1,0:T(8,128)(2,1)}, bf16[2048,1024]{1,0:T(8,128)(2,1)}, u32[]{:S(2)}, u32[]{:S(2)}) %collective-permute-start.15) | collective-permute-done | bytes 4194336 | tf_op jit(solution)/shard_map/ppermute | solution.py:56
  296.1 44.2 %collective-permute-done.16.refs_9_.refs_2_ = bf16[2048,512]{1,0:T(8,128)(2,1)} collective-permute-done((bf16[2048,512]{1,0:T(8,128)(2,1)S(1)}, bf16[2048,512]{1,0:T(8,128)(2,1)}, u32[]{:S(2)}, u32[]{:S(2)}) %collective-permute-start.16) | collective-permute-done | bytes 2097184 | tf_op jit(solution)/shard_map/ppermute | solution.py:56
  340.2 17.8 %shard_map.173 = (bf16[768,1024]{1,0:T(8,128)(2,1)}, bf16[768,1024]{1,0:T(8,128)(2,1)}, bf16[768,1024]{1,0:T(8,128)(2,1)}, f32[768,128]{1,0:T(8,128)}) custom-call(s32[1]{0:T(128)} %bitcast.8.index_ref, bf16[384,2176]{1,0:T(8,128)(2,1)} %constant_dynamic-update-slice_fusion.refs_0_, bf16[384,2176]{1,0:T(8,128)(2,1)} %collective-permute-done.22.refs_1_, ...), custom_call_target="tpu_custom_call" | custom-call | flops 9663676416 | bytes 12582912 | tf_op jit(solution)/shard_map/pallas_call | solution.py:198
  358.1 12.2 %shard_map.174 = bf16[384,4096]{1,0:T(8,128)(2,1)} custom-call(bf16[768,1024]{1,0:T(8,128)(2,1)} %get-tuple-element.39.act_ref, bf16[768,1024]{1,0:T(8,128)(2,1)} %get-tuple-element.40.dgate_ref, bf16[768,1024]{1,0:T(8,128)(2,1)} %get-tuple-element.41.dup_ref, bf16[2048,512]{1,0:T(8,128)(2,1)} %bitcast.203, ...), custom_call_target="tpu_custom_call" | custom-call | flops 4831838208 | bytes 18874368 | tf_op jit(solution)/shard_map/pallas_call | solution.py:275
  374.1 17.8 %shard_map.170 = (bf16[768,1024]{1,0:T(8,128)(2,1)}, bf16[768,1024]{1,0:T(8,128)(2,1)}, bf16[768,1024]{1,0:T(8,128)(2,1)}, f32[768,128]{1,0:T(8,128)}) custom-call(s32[1]{0:T(128)} %bitcast.8.index_ref, bf16[384,2176]{1,0:T(8,128)(2,1)} %pad_maximum_fusion.8.refs_0_, bf16[384,2176]{1,0:T(8,128)(2,1)} %collective-permute-done.10.refs_1_, ...), custom_call_target="tpu_custom_call" | custom-call | flops 9663676416 | bytes 12582912 | tf_op jit(solution)/shard_map/pallas_call | solution.py:198
  393.1 12.5 %shard_map.171 = bf16[384,4096]{1,0:T(8,128)(2,1)} custom-call(bf16[768,1024]{1,0:T(8,128)(2,1)} %get-tuple-element.35.act_ref, bf16[768,1024]{1,0:T(8,128)(2,1)} %get-tuple-element.36.dgate_ref, bf16[768,1024]{1,0:T(8,128)(2,1)} %get-tuple-element.37.dup_ref, bf16[2048,512]{1,0:T(8,128)(2,1)} %bitcast.205, ...), custom_call_target="tpu_custom_call" | custom-call | flops 4831838208 | bytes 18874368 | tf_op jit(solution)/shard_map/pallas_call | solution.py:275
  411.5 7.5 all-to-all-start
  427.9 12.9 %shard_map.175 = (bf16[96,4096]{1,0:T(8,128)(2,1)}, bf16[96,4096]{1,0:T(8,128)(2,1)}, bf16[96,4096]{1,0:T(8,128)(2,1)}, bf16[96,4096]{1,0:T(8,128)(2,1)}) custom-call(bf16[768,1024]{1,0:T(8,128)(2,1)} %get-tuple-element.39.act_ref, bf16[768,1024]{1,0:T(8,128)(2,1)} %get-tuple-element.40.dgate_ref, bf16[768,1024]{1,0:T(8,128)(2,1)} %get-tuple-element.41.dup_ref, ...), custom_call_target="tpu_custom_call" | custom-call | flops 4831838208 | bytes 18874368 | tf_op jit(solution)/shard_map/pallas_call | solution.py:275
  442.8 12.4 %convolution_convert_fusion = bf16[2048,1024]{1,0:T(8,128)(2,1)} fusion(bf16[1536,512]{1,0:T(8,128)(2,1)S(1)} %copy-done.43, bf16[1536,512]{1,0:T(8,128)(2,1)} %slice.209, bf16[384,2176]{1,0:T(8,128)(2,1)} %collective-permute-done.22.refs_1_, bf16[384,2176]{1,0:T(8,128)(2,1)} %constant_dynamic-update-slice_fusion.refs_0_, ...), kind=kOutput, calls=%fused_computation.20 | convolution fusion | flops 6494879744 | bytes 14024704 | tf_op jit(solution)/shard_map/dot_general | solution.py:486
  458.3 12.7 %shard_map.172 = (bf16[96,4096]{1,0:T(8,128)(2,1)}, bf16[96,4096]{1,0:T(8,128)(2,1)}, bf16[96,4096]{1,0:T(8,128)(2,1)}, bf16[96,4096]{1,0:T(8,128)(2,1)}) custom-call(bf16[768,1024]{1,0:T(8,128)(2,1)} %get-tuple-element.35.act_ref, bf16[768,1024]{1,0:T(8,128)(2,1)} %get-tuple-element.36.dgate_ref, bf16[768,1024]{1,0:T(8,128)(2,1)} %get-tuple-element.37.dup_ref, ...), custom_call_target="tpu_custom_call" | custom-call | flops 4831838208 | bytes 18874368 | tf_op jit(solution)/shard_map/pallas_call | solution.py:275
  477.2 14.5 %collective-permute-done.32 = bf16[96,4096]{1,0:T(8,128)(2,1)S(1)} collective-permute-done((bf16[96,4096]{1,0:T(8,128)(2,1)}, bf16[96,4096]{1,0:T(8,128)(2,1)S(1)}, u32[]{:S(2)}, u32[]{:S(2)}) %collective-permute-start.32) | collective-permute-done | bytes 786464 | tf_op jit(solution)/shard_map/ppermute | solution.py:60
  496.3 12.3 %collective-permute-done.30 = bf16[96,4096]{1,0:T(8,128)(2,1)S(1)} collective-permute-done((bf16[96,4096]{1,0:T(8,128)(2,1)}, bf16[96,4096]{1,0:T(8,128)(2,1)S(1)}, u32[]{:S(2)}, u32[]{:S(2)}) %collective-permute-start.30) | collective-permute-done | bytes 786464 | tf_op jit(solution)/shard_map/ppermute | solution.py:60
  512.9 6.9 convolution_convert_fusion.2
  524.1 6.0 collective-permute-done.33
  530.1 12.7 %collective-permute-done.31 = bf16[96,4096]{1,0:T(8,128)(2,1)} collective-permute-done((bf16[96,4096]{1,0:T(8,128)(2,1)}, bf16[96,4096]{1,0:T(8,128)(2,1)}, u32[]{:S(2)}, u32[]{:S(2)}) %collective-permute-start.31) | collective-permute-done | bytes 786464 | tf_op jit(solution)/shard_map/ppermute | solution.py:65
  548.6 9.1 add_bitcast_fusion.1
  587.5 8.9 add_bitcast_fusion.2
  597.1 4.4 maximum_bitcast_fusion
  601.6 16.5 %copy.135 = f32[1,2048,2,512]{3,2,1,0:T(2,128)} copy(f32[1,2048,2,512]{3,1,2,0:T(8,128)S(1)} %maximum_bitcast_fusion) | data formatting | bytes 16777216
  618.1 107.3 %all-reduce.4.cloned.1.call-done = f32[17,2048]{1,0:T(8,128)} async-done(((f32[17,2048]{1,0:T(8,128)}), f32[17,2048]{1,0:T(8,128)}) %all-reduce.4.cloned.1.call-update) | async-done | bytes 139280 | tf_op jit(solution)/shard_map/psum | solution.py:623
  732.5 14.9 %collective-permute-done.39 = bf16[192,2048]{1,0:T(8,128)(2,1)S(1)} collective-permute-done((bf16[192,2048]{1,0:T(8,128)(2,1)S(1)}, bf16[192,2048]{1,0:T(8,128)(2,1)S(1)}, u32[]{:S(2)}, u32[]{:S(2)}) %collective-permute-start.39) | collective-permute-done | bytes 786464 | tf_op jit(solution)/shard_map/ppermute | solution.py:60
  753.1 5.1 all-reduce
  764.1 3.8 fusion.17
  775.2 5.3 shard_map.178
  785.0 5.3 shard_map.176
  792.2 4.3 convolution_convert_fusion.1
  812.7 52.5 %collective-permute-done.36 = bf16[96,2048]{1,0:T(8,128)(2,1)S(1)} collective-permute-done((bf16[96,2048]{1,0:T(8,128)(2,1)S(1)}, bf16[96,2048]{1,0:T(8,128)(2,1)S(1)}, u32[]{:S(2)}, u32[]{:S(2)}) %collective-permute-start.36) | collective-permute-done | bytes 393248 | tf_op jit(solution)/shard_map/ppermute | solution.py:56
  866.3 6.8 shard_map.179
  875.1 4.1 collective-permute-done.41
  883.8 6.8 shard_map.177
  899.5 11.1 %collective-permute-done.47 = bf16[384,1024]{1,0:T(8,128)(2,1)S(1)} collective-permute-done((bf16[384,1024]{1,0:T(8,128)(2,1)}, bf16[384,1024]{1,0:T(8,128)(2,1)S(1)}, u32[]{:S(2)}, u32[]{:S(2)}) %collective-permute-start.47) | collective-permute-done | bytes 786464 | tf_op jit(solution)/shard_map/ppermute | solution.py:60
  915.0 12.5 %collective-permute-done.45 = bf16[384,1024]{1,0:T(8,128)(2,1)S(1)} collective-permute-done((bf16[384,1024]{1,0:T(8,128)(2,1)}, bf16[384,1024]{1,0:T(8,128)(2,1)S(1)}, u32[]{:S(2)}, u32[]{:S(2)}) %collective-permute-start.45) | collective-permute-done | bytes 786464 | tf_op jit(solution)/shard_map/ppermute | solution.py:60
  931.5 7.2 add_bitcast_fusion
  940.5 22.6 %collective-permute-done.48 = bf16[384,1024]{1,0:T(8,128)(2,1)} collective-permute-done((bf16[384,1024]{1,0:T(8,128)(2,1)}, bf16[384,1024]{1,0:T(8,128)(2,1)}, u32[]{:S(2)}, u32[]{:S(2)}) %collective-permute-start.48) | collective-permute-done | bytes 786464 | tf_op jit(solution)/shard_map/ppermute | solution.py:65
  (501 shorter events, 242.5 us)
Async XLA Ops:
  7.2 123.1 %all-gather.3.cloned.1.call-start = ((), (), s32[]{:S(2)}) async-start(), calls=%async_computation.2 | async-start | bytes 13369344 | tf_op jit(solution)/shard_map/all_gather | solution.py:340
  8.0 181.0 %all-gather.5.cloned.1.call-start = ((), (), s32[]{:S(2)}) async-start(), calls=%async_computation.3 | async-start | bytes 4456448 | tf_op jit(solution)/shard_map/all_gather | solution.py:341
  9.8 202.7 %collective-permute-start.23 = (bf16[96,2048]{1,0:T(8,128)(2,1)}, bf16[96,2048]{1,0:T(8,128)(2,1)}, u32[]{:S(2)}, u32[]{:S(2)}) collective-permute-start(bf16[96,2048]{1,0:T(8,128)(2,1)} %constant_dynamic-slice_fusion), channel_id=1, source_target_pairs={{0,4},{2,6},{4,0},{6,2},{1,5},{3,7},{5,1},{7,3},{8,12},{10,14},{12... | collective-permute-start | bytes 1179656 | tf_op jit(solution)/shard_map/ppermute | solution.py:60
  12.8 187.4 %collective-permute-start.11 = (bf16[96,2048]{1,0:T(8,128)(2,1)}, bf16[96,2048]{1,0:T(8,128)(2,1)}, u32[]{:S(2)}, u32[]{:S(2)}) collective-permute-start(bf16[96,2048]{1,0:T(8,128)(2,1)} %constant_dynamic-slice_fusion), channel_id=1, source_target_pairs={{0,8},{8,16},{16,24},{24,0},{1,9},{9,17},{17,25},{25,1},{2,10},{10... | collective-permute-start | bytes 1179656 | tf_op jit(solution)/shard_map/ppermute | solution.py:65
  14.3 186.4 %collective-permute-start.12 = (bf16[96,2048]{1,0:T(8,128)(2,1)}, bf16[96,2048]{1,0:T(8,128)(2,1)}, u32[]{:S(2)}, u32[]{:S(2)}) collective-permute-start(bf16[96,2048]{1,0:T(8,128)(2,1)} %constant_dynamic-slice_fusion), channel_id=1, source_target_pairs={{0,16},{8,24},{16,0},{24,8},{1,17},{9,25},{17,1},{25,9},{2,18},{10... | collective-permute-start | bytes 1179656 | tf_op jit(solution)/shard_map/ppermute | solution.py:65
  149.7 22.1 %collective-permute-start.1 = (bf16[192,1024]{1,0:T(8,128)(2,1)S(1)}, bf16[192,1024]{1,0:T(8,128)(2,1)S(1)}, u32[]{:S(2)}, u32[]{:S(2)}) collective-permute-start(bf16[192,1024]{1,0:T(8,128)(2,1)S(1)} %fusion.46), channel_id=1, source_target_pairs={{0,4},{2,6},{4,0},{6,2},{1,5},{3,7},{5,1},{7,3},{8,12},{10,14},{12... | collective-permute-start | bytes 1179656 | tf_op jit(solution)/shard_map/ppermute | solution.py:60
  157.8 14.0 %collective-permute-start.5 = (bf16[192,1024]{1,0:T(8,128)(2,1)S(1)}, bf16[192,1024]{1,0:T(8,128)(2,1)S(1)}, u32[]{:S(2)}, u32[]{:S(2)}) collective-permute-start(bf16[192,1024]{1,0:T(8,128)(2,1)S(1)} %collective-permute-done.4), channel_id=1, source_target_pairs={{0,2},{2,0},{4,6},{6,4},{1,3},{3,1},{5,7},{7,5},{8,10},{10,8},{12,... | collective-permute-start | bytes 1179656 | tf_op jit(solution)/shard_map/ppermute | solution.py:60
  175.1 43.2 %collective-permute-start.13 = (bf16[96,2048]{1,0:T(8,128)(2,1)}, bf16[96,2048]{1,0:T(8,128)(2,1)}, u32[]{:S(2)}, u32[]{:S(2)}) collective-permute-start(bf16[96,2048]{1,0:T(8,128)(2,1)} %constant_dynamic-slice_fusion), channel_id=1, source_target_pairs={{0,24},{8,0},{16,8},{24,16},{1,25},{9,1},{17,9},{25,17},{2,26},{10... | collective-permute-start | bytes 1179656 | tf_op jit(solution)/shard_map/ppermute | solution.py:65
  200.2 95.9 %collective-permute-start.15 = (bf16[2048,1024]{1,0:T(8,128)(2,1)}, bf16[2048,1024]{1,0:T(8,128)(2,1)}, u32[]{:S(2)}, u32[]{:S(2)}) collective-permute-start(bf16[2048,1024]{1,0:T(8,128)(2,1)} %pad_maximum_fusion.7.refs_4_.refs_5_.refs_1_), channel_id=1, source_target_pairs={{0,1},{1,0},{2,3},{3,2},{4,5},{5,4},{6,7},{7,6},{8,9},{9,8},{10,11... | collective-permute-start | bytes 12582920 | tf_op jit(solution)/shard_map/ppermute | solution.py:56
  200.7 19.0 %collective-permute-start.24 = (bf16[96,2048]{1,0:T(8,128)(2,1)}, bf16[96,2048]{1,0:T(8,128)(2,1)}, u32[]{:S(2)}, u32[]{:S(2)}) collective-permute-start(bf16[96,2048]{1,0:T(8,128)(2,1)} %collective-permute-done.11), channel_id=1, source_target_pairs={{0,4},{2,6},{4,0},{6,2},{1,5},{3,7},{5,1},{7,3},{8,12},{10,14},{12... | collective-permute-start | bytes 1179656 | tf_op jit(solution)/shard_map/ppermute | solution.py:60
  206.8 17.1 %collective-permute-start.25 = (bf16[96,2048]{1,0:T(8,128)(2,1)}, bf16[96,2048]{1,0:T(8,128)(2,1)}, u32[]{:S(2)}, u32[]{:S(2)}) collective-permute-start(bf16[96,2048]{1,0:T(8,128)(2,1)} %collective-permute-done.12), channel_id=1, source_target_pairs={{0,4},{2,6},{4,0},{6,2},{1,5},{3,7},{5,1},{7,3},{8,12},{10,14},{12... | collective-permute-start | bytes 1179656 | tf_op jit(solution)/shard_map/ppermute | solution.py:60
  212.5 16.5 %collective-permute-start.7 = (bf16[96,2176]{1,0:T(8,128)(2,1)}, bf16[96,2176]{1,0:T(8,128)(2,1)S(1)}, u32[]{:S(2)}, u32[]{:S(2)}) collective-permute-start(bf16[96,2176]{1,0:T(8,128)(2,1)} %concatenate.122), channel_id=1, source_target_pairs={{0,8},{8,16},{16,24},{24,0},{1,9},{9,17},{17,25},{25,1},{2,10},{10... | collective-permute-start | bytes 1253384 | tf_op jit(solution)/shard_map/ppermute | solution.py:65
  219.7 24.9 %collective-permute-start.8 = (bf16[96,2176]{1,0:T(8,128)(2,1)}, bf16[96,2176]{1,0:T(8,128)(2,1)S(1)}, u32[]{:S(2)}, u32[]{:S(2)}) collective-permute-start(bf16[96,2176]{1,0:T(8,128)(2,1)} %concatenate.122), channel_id=1, source_target_pairs={{0,16},{8,24},{16,0},{24,8},{1,17},{9,25},{17,1},{25,9},{2,18},{10... | collective-permute-start | bytes 1253384 | tf_op jit(solution)/shard_map/ppermute | solution.py:65
  223.9 23.2 %collective-permute-start.9 = (bf16[96,2176]{1,0:T(8,128)(2,1)}, bf16[96,2176]{1,0:T(8,128)(2,1)S(1)}, u32[]{:S(2)}, u32[]{:S(2)}) collective-permute-start(bf16[96,2176]{1,0:T(8,128)(2,1)} %concatenate.122), channel_id=1, source_target_pairs={{0,24},{8,0},{16,8},{24,16},{1,25},{9,1},{17,9},{25,17},{2,26},{10... | collective-permute-start | bytes 1253384 | tf_op jit(solution)/shard_map/ppermute | solution.py:65
  229.0 19.6 %collective-permute-start.19 = (bf16[96,2176]{1,0:T(8,128)(2,1)S(1)}, bf16[96,2176]{1,0:T(8,128)(2,1)S(1)}, u32[]{:S(2)}, u32[]{:S(2)}) collective-permute-start(bf16[96,2176]{1,0:T(8,128)(2,1)S(1)} %collective-permute-done.7), channel_id=1, source_target_pairs={{0,4},{2,6},{4,0},{6,2},{1,5},{3,7},{5,1},{7,3},{8,12},{10,14},{12... | collective-permute-start | bytes 1253384 | tf_op jit(solution)/shard_map/ppermute | solution.py:60
  232.3 33.5 %collective-permute-start.26 = (bf16[96,2048]{1,0:T(8,128)(2,1)}, bf16[96,2048]{1,0:T(8,128)(2,1)S(1)}, u32[]{:S(2)}, u32[]{:S(2)}) collective-permute-start(bf16[96,2048]{1,0:T(8,128)(2,1)} %collective-permute-done.13), channel_id=1, source_target_pairs={{0,4},{2,6},{4,0},{6,2},{1,5},{3,7},{5,1},{7,3},{8,12},{10,14},{12... | collective-permute-start | bytes 1179656 | tf_op jit(solution)/shard_map/ppermute | solution.py:60
  247.1 93.2 %collective-permute-start.16 = (bf16[2048,512]{1,0:T(8,128)(2,1)S(1)}, bf16[2048,512]{1,0:T(8,128)(2,1)}, u32[]{:S(2)}, u32[]{:S(2)}) collective-permute-start(bf16[2048,512]{1,0:T(8,128)(2,1)S(1)} %bitcast.208), channel_id=1, source_target_pairs={{0,1},{1,0},{2,3},{3,2},{4,5},{5,4},{6,7},{7,6},{8,9},{9,8},{10,11... | collective-permute-start | bytes 6291464 | tf_op jit(solution)/shard_map/ppermute | solution.py:56
  248.6 16.5 %collective-permute-start.21 = (bf16[96,2176]{1,0:T(8,128)(2,1)S(1)}, bf16[96,2176]{1,0:T(8,128)(2,1)S(1)}, u32[]{:S(2)}, u32[]{:S(2)}) collective-permute-start(bf16[96,2176]{1,0:T(8,128)(2,1)S(1)} %collective-permute-done.9), channel_id=1, source_target_pairs={{0,4},{2,6},{4,0},{6,2},{1,5},{3,7},{5,1},{7,3},{8,12},{10,14},{12... | collective-permute-start | bytes 1253384 | tf_op jit(solution)/shard_map/ppermute | solution.py:60
  265.9 74.4 %collective-permute-start.22 = (bf16[384,2176]{1,0:T(8,128)(2,1)}, bf16[384,2176]{1,0:T(8,128)(2,1)}, u32[]{:S(2)}, u32[]{:S(2)}) collective-permute-start(bf16[384,2176]{1,0:T(8,128)(2,1)} %constant_dynamic-update-slice_fusion.refs_0_), channel_id=1, source_target_pairs={{0,2},{2,0},{4,6},{6,4},{1,3},{3,1},{5,7},{7,5},{8,10},{10,8},{12,... | collective-permute-start | bytes 5013512 | tf_op jit(solution)/shard_map/ppermute | solution.py:60
  270.0 104.0 %collective-permute-start.14 = (bf16[384,2048]{1,0:T(8,128)(2,1)}, bf16[384,2048]{1,0:T(8,128)(2,1)}, u32[]{:S(2)}, u32[]{:S(2)}) collective-permute-start(bf16[384,2048]{1,0:T(8,128)(2,1)} %pad_maximum_fusion.9.refs_2_), channel_id=1, source_target_pairs={{0,2},{2,0},{4,6},{6,4},{1,3},{3,1},{5,7},{7,5},{8,10},{10,8},{12,... | collective-permute-start | bytes 4718600 | tf_op jit(solution)/shard_map/ppermute | solution.py:60
  272.0 102.0 %collective-permute-start.10 = (bf16[384,2176]{1,0:T(8,128)(2,1)}, bf16[384,2176]{1,0:T(8,128)(2,1)}, u32[]{:S(2)}, u32[]{:S(2)}) collective-permute-start(bf16[384,2176]{1,0:T(8,128)(2,1)} %pad_maximum_fusion.8.refs_0_), channel_id=1, source_target_pairs={{0,2},{2,0},{4,6},{6,4},{1,3},{3,1},{5,7},{7,5},{8,10},{10,8},{12,... | collective-permute-start | bytes 5013512 | tf_op jit(solution)/shard_map/ppermute | solution.py:60
  370.4 57.5 %collective-permute-start.28 = (bf16[384,4096]{1,0:T(8,128)(2,1)}, bf16[384,4096]{1,0:T(8,128)(2,1)}, u32[]{:S(2)}, u32[]{:S(2)}) collective-permute-start(bf16[384,4096]{1,0:T(8,128)(2,1)} %shard_map.174), channel_id=1, source_target_pairs={{0,2},{2,0},{4,6},{6,4},{1,3},{3,1},{5,7},{7,5},{8,10},{10,8},{12,... | collective-permute-start | bytes 9437192 | tf_op jit(solution)/shard_map/ppermute | solution.py:60
  405.6 52.7 %collective-permute-start.17 = (bf16[384,4096]{1,0:T(8,128)(2,1)}, bf16[384,4096]{1,0:T(8,128)(2,1)}, u32[]{:S(2)}, u32[]{:S(2)}) collective-permute-start(bf16[384,4096]{1,0:T(8,128)(2,1)} %shard_map.171), channel_id=1, source_target_pairs={{0,2},{2,0},{4,6},{6,4},{1,3},{3,1},{5,7},{7,5},{8,10},{10,8},{12,... | collective-permute-start | bytes 9437192 | tf_op jit(solution)/shard_map/ppermute | solution.py:60
  411.5 108.3 %all-to-all-start = ((f32[16,1,96]{2,1,0:T(1,128)}), f32[16,1,96]{2,1,0:T(1,128)S(1)}, u32[]{:S(2)}, u32[]{:S(2)}) async-start(f32[16,1,96]{2,1,0:T(1,128)} %bitcast.15), calls=%async_computation | async-start | bytes 16384 | tf_op jit(solution)/shard_map/all_to_all | solution.py:511
  419.0 306.4 %all-reduce.4.cloned.1.call-start = ((), (), s32[]{:S(2)}) async-start(), calls=%async_computation.5 | async-start | bytes 393216 | tf_op jit(solution)/shard_map/psum | solution.py:623
  440.8 32.6 %collective-permute-start.34 = (bf16[96,4096]{1,0:T(8,128)(2,1)}, bf16[96,4096]{1,0:T(8,128)(2,1)}, u32[]{:S(2)}, u32[]{:S(2)}) collective-permute-start(bf16[96,4096]{1,0:T(8,128)(2,1)} %get-tuple-element.48), channel_id=1, source_target_pairs={{0,4},{2,6},{4,0},{6,2},{1,5},{3,7},{5,1},{7,3},{8,12},{10,14},{12... | collective-permute-start | bytes 2359304 | tf_op jit(solution)/shard_map/ppermute | solution.py:60
  455.1 93.4 %collective-permute-start.57 = (bf16[2048,1024]{1,0:T(8,128)(2,1)}, bf16[2048,1024]{1,0:T(8,128)(2,1)}, u32[]{:S(2)}, u32[]{:S(2)}) collective-permute-start(bf16[2048,1024]{1,0:T(8,128)(2,1)} %convolution_convert_fusion), channel_id=1, source_target_pairs={{0,1},{1,0},{2,3},{3,2},{4,5},{5,4},{6,7},{7,6},{8,9},{9,8},{10,11... | collective-permute-start | bytes 12582920 | tf_op jit(solution)/shard_map/ppermute | solution.py:56
  471.0 20.7 %collective-permute-start.32 = (bf16[96,4096]{1,0:T(8,128)(2,1)}, bf16[96,4096]{1,0:T(8,128)(2,1)S(1)}, u32[]{:S(2)}, u32[]{:S(2)}) collective-permute-start(bf16[96,4096]{1,0:T(8,128)(2,1)} %get-tuple-element.46), channel_id=1, source_target_pairs={{0,4},{2,6},{4,0},{6,2},{1,5},{3,7},{5,1},{7,3},{8,12},{10,14},{12... | collective-permute-start | bytes 2359304 | tf_op jit(solution)/shard_map/ppermute | solution.py:60
  471.3 37.2 %collective-permute-start.30 = (bf16[96,4096]{1,0:T(8,128)(2,1)}, bf16[96,4096]{1,0:T(8,128)(2,1)S(1)}, u32[]{:S(2)}, u32[]{:S(2)}) collective-permute-start(bf16[96,4096]{1,0:T(8,128)(2,1)} %get-tuple-element.44), channel_id=1, source_target_pairs={{0,4},{2,6},{4,0},{6,2},{1,5},{3,7},{5,1},{7,3},{8,12},{10,14},{12... | collective-permute-start | bytes 2359304 | tf_op jit(solution)/shard_map/ppermute | solution.py:60
  473.1 51.0 %collective-permute-start.29 = (bf16[96,4096]{1,0:T(8,128)(2,1)}, bf16[96,4096]{1,0:T(8,128)(2,1)}, u32[]{:S(2)}, u32[]{:S(2)}) collective-permute-start(bf16[96,4096]{1,0:T(8,128)(2,1)} %get-tuple-element.42), channel_id=1, source_target_pairs={{0,4},{2,6},{4,0},{6,2},{1,5},{3,7},{5,1},{7,3},{8,12},{10,14},{12... | collective-permute-start | bytes 2359304 | tf_op jit(solution)/shard_map/ppermute | solution.py:60
  475.1 49.0 %collective-permute-start.35 = (bf16[96,4096]{1,0:T(8,128)(2,1)S(1)}, bf16[96,4096]{1,0:T(8,128)(2,1)}, u32[]{:S(2)}, u32[]{:S(2)}) collective-permute-start(bf16[96,4096]{1,0:T(8,128)(2,1)S(1)} %add_convert_fusion.4), channel_id=1, source_target_pairs={{0,8},{8,16},{16,24},{24,0},{1,9},{9,17},{17,25},{25,1},{2,10},{10... | collective-permute-start | bytes 2359304 | tf_op jit(solution)/shard_map/ppermute | solution.py:65
  493.9 36.2 %collective-permute-start.33 = (bf16[96,4096]{1,0:T(8,128)(2,1)}, bf16[96,4096]{1,0:T(8,128)(2,1)}, u32[]{:S(2)}, u32[]{:S(2)}) collective-permute-start(bf16[96,4096]{1,0:T(8,128)(2,1)} %add_convert_fusion.5), channel_id=1, source_target_pairs={{0,16},{8,24},{16,0},{24,8},{1,17},{9,25},{17,1},{25,9},{2,18},{10... | collective-permute-start | bytes 2359304 | tf_op jit(solution)/shard_map/ppermute | solution.py:65
  509.7 33.1 %collective-permute-start.31 = (bf16[96,4096]{1,0:T(8,128)(2,1)}, bf16[96,4096]{1,0:T(8,128)(2,1)}, u32[]{:S(2)}, u32[]{:S(2)}) collective-permute-start(bf16[96,4096]{1,0:T(8,128)(2,1)} %add_convert_fusion.6), channel_id=1, source_target_pairs={{0,24},{8,0},{16,8},{24,16},{1,25},{9,1},{17,9},{25,17},{2,26},{10... | collective-permute-start | bytes 2359304 | tf_op jit(solution)/shard_map/ppermute | solution.py:65
  587.3 139.7 %collective-permute-start.38 = (bf16[2,192,2048]{2,1,0:T(8,128)(2,1)}, bf16[2,192,2048]{2,1,0:T(8,128)(2,1)}, u32[]{:S(2)}, u32[]{:S(2)}) collective-permute-start(bf16[2,192,2048]{2,1,0:T(8,128)(2,1)} %pad_maximum_fusion.10), channel_id=1, source_target_pairs={{0,2},{2,0},{4,6},{6,4},{1,3},{3,1},{5,7},{7,5},{8,10},{10,8},{12,... | collective-permute-start | bytes 4718600 | tf_op jit(solution)/shard_map/ppermute | solution.py:60
  597.1 341.6 %reduce-scatter.2.cloned.1.call-start = ((), (), s32[]{:S(2)}) async-start(), calls=%async_computation.4 | async-start | bytes 4456448 | tf_op jit(solution)/shard_map/reduce_scatter | solution.py:537
  728.7 18.7 %collective-permute-start.39 = (bf16[192,2048]{1,0:T(8,128)(2,1)S(1)}, bf16[192,2048]{1,0:T(8,128)(2,1)S(1)}, u32[]{:S(2)}, u32[]{:S(2)}) collective-permute-start(bf16[192,2048]{1,0:T(8,128)(2,1)S(1)} %fusion.53), channel_id=1, source_target_pairs={{0,4},{2,6},{4,0},{6,2},{1,5},{3,7},{5,1},{7,3},{8,12},{10,14},{12... | collective-permute-start | bytes 2359304 | tf_op jit(solution)/shard_map/ppermute | solution.py:60
  780.6 85.7 %collective-permute-start.43 = (bf16[4,384,1024]{2,1,0:T(8,128)(2,1)}, bf16[4,384,1024]{2,1,0:T(8,128)(2,1)}, u32[]{:S(2)}, u32[]{:S(2)}) collective-permute-start(bf16[4,384,1024]{2,1,0:T(8,128)(2,1)} %shard_map.178), channel_id=1, source_target_pairs={{0,2},{2,0},{4,6},{6,4},{1,3},{3,1},{5,7},{7,5},{8,10},{10,8},{12,... | collective-permute-start | bytes 9437192 | tf_op jit(solution)/shard_map/ppermute | solution.py:60
  790.3 93.3 %collective-permute-start.42 = (bf16[4,384,1024]{2,1,0:T(8,128)(2,1)}, bf16[4,384,1024]{2,1,0:T(8,128)(2,1)}, u32[]{:S(2)}, u32[]{:S(2)}) collective-permute-start(bf16[4,384,1024]{2,1,0:T(8,128)(2,1)} %shard_map.176), channel_id=1, source_target_pairs={{0,2},{2,0},{4,6},{6,4},{1,3},{3,1},{5,7},{7,5},{8,10},{10,8},{12,... | collective-permute-start | bytes 9437192 | tf_op jit(solution)/shard_map/ppermute | solution.py:60
  808.1 123.4 %collective-permute-start.58 = (bf16[2048,512]{1,0:T(8,128)(2,1)}, bf16[2048,512]{1,0:T(8,128)(2,1)}, u32[]{:S(2)}, u32[]{:S(2)}) collective-permute-start(bf16[2048,512]{1,0:T(8,128)(2,1)} %convolution_convert_fusion.2), channel_id=1, source_target_pairs={{0,1},{1,0},{2,3},{3,2},{4,5},{5,4},{6,7},{7,6},{8,9},{9,8},{10,11... | collective-permute-start | bytes 6291464 | tf_op jit(solution)/shard_map/ppermute | solution.py:56
  810.0 55.3 %collective-permute-start.36 = (bf16[96,2048]{1,0:T(8,128)(2,1)S(1)}, bf16[96,2048]{1,0:T(8,128)(2,1)S(1)}, u32[]{:S(2)}, u32[]{:S(2)}) collective-permute-start(bf16[96,2048]{1,0:T(8,128)(2,1)S(1)} %get-tuple-element.120), channel_id=1, source_target_pairs={{0,1},{1,0},{2,3},{3,2},{4,5},{5,4},{6,7},{7,6},{8,9},{9,8},{10,11... | collective-permute-start | bytes 1179656 | tf_op jit(solution)/shard_map/ppermute | solution.py:56
  810.7 68.5 %collective-permute-start.41 = (f32[96,2048]{1,0:T(8,128)}, f32[96,2048]{1,0:T(8,128)S(1)}, u32[]{:S(2)}, u32[]{:S(2)}) collective-permute-start(f32[96,2048]{1,0:T(8,128)} %get-tuple-element.119), channel_id=1, source_target_pairs={{0,1},{1,0},{2,3},{3,2},{4,5},{5,4},{6,7},{7,6},{8,9},{9,8},{10,11... | collective-permute-start | bytes 2359304 | tf_op jit(solution)/shard_map/ppermute | solution.py:56
  873.1 20.6 %collective-permute-start.49 = (bf16[384,1024]{1,0:T(8,128)(2,1)}, bf16[384,1024]{1,0:T(8,128)(2,1)S(1)}, u32[]{:S(2)}, u32[]{:S(2)}) collective-permute-start(bf16[384,1024]{1,0:T(8,128)(2,1)} %get-tuple-element.58), channel_id=1, source_target_pairs={{0,4},{2,6},{4,0},{6,2},{1,5},{3,7},{5,1},{7,3},{8,12},{10,14},{12... | collective-permute-start | bytes 2359304 | tf_op jit(solution)/shard_map/ppermute | solution.py:60
  874.5 36.0 %collective-permute-start.47 = (bf16[384,1024]{1,0:T(8,128)(2,1)}, bf16[384,1024]{1,0:T(8,128)(2,1)S(1)}, u32[]{:S(2)}, u32[]{:S(2)}) collective-permute-start(bf16[384,1024]{1,0:T(8,128)(2,1)} %get-tuple-element.56), channel_id=1, source_target_pairs={{0,4},{2,6},{4,0},{6,2},{1,5},{3,7},{5,1},{7,3},{8,12},{10,14},{12... | collective-permute-start | bytes 2359304 | tf_op jit(solution)/shard_map/ppermute | solution.py:60
  880.4 47.0 %collective-permute-start.45 = (bf16[384,1024]{1,0:T(8,128)(2,1)}, bf16[384,1024]{1,0:T(8,128)(2,1)S(1)}, u32[]{:S(2)}, u32[]{:S(2)}) collective-permute-start(bf16[384,1024]{1,0:T(8,128)(2,1)} %get-tuple-element.54), channel_id=1, source_target_pairs={{0,4},{2,6},{4,0},{6,2},{1,5},{3,7},{5,1},{7,3},{8,12},{10,14},{12... | collective-permute-start | bytes 2359304 | tf_op jit(solution)/shard_map/ppermute | solution.py:60
  883.6 56.9 %collective-permute-start.44 = (bf16[384,1024]{1,0:T(8,128)(2,1)}, bf16[384,1024]{1,0:T(8,128)(2,1)}, u32[]{:S(2)}, u32[]{:S(2)}) collective-permute-start(bf16[384,1024]{1,0:T(8,128)(2,1)} %get-tuple-element.52), channel_id=1, source_target_pairs={{0,4},{2,6},{4,0},{6,2},{1,5},{3,7},{5,1},{7,3},{8,12},{10,14},{12... | collective-permute-start | bytes 2359304 | tf_op jit(solution)/shard_map/ppermute | solution.py:60
  896.5 44.0 %collective-permute-start.50 = (bf16[384,1024]{1,0:T(8,128)(2,1)S(1)}, bf16[384,1024]{1,0:T(8,128)(2,1)}, u32[]{:S(2)}, u32[]{:S(2)}) collective-permute-start(bf16[384,1024]{1,0:T(8,128)(2,1)S(1)} %add_convert_fusion), channel_id=1, source_target_pairs={{0,24},{8,0},{16,8},{24,16},{1,25},{9,1},{17,9},{25,17},{2,26},{10... | collective-permute-start | bytes 2359304 | tf_op jit(solution)/shard_map/ppermute | solution.py:65
  913.0 50.1 %collective-permute-start.48 = (bf16[384,1024]{1,0:T(8,128)(2,1)}, bf16[384,1024]{1,0:T(8,128)(2,1)}, u32[]{:S(2)}, u32[]{:S(2)}) collective-permute-start(bf16[384,1024]{1,0:T(8,128)(2,1)} %add_convert_fusion.1), channel_id=1, source_target_pairs={{0,16},{8,24},{16,0},{24,8},{1,17},{9,25},{17,1},{25,9},{2,18},{10... | collective-permute-start | bytes 2359304 | tf_op jit(solution)/shard_map/ppermute | solution.py:65
  927.7 35.3 %collective-permute-start.46 = (bf16[384,1024]{1,0:T(8,128)(2,1)S(1)}, bf16[384,1024]{1,0:T(8,128)(2,1)}, u32[]{:S(2)}, u32[]{:S(2)}) collective-permute-start(bf16[384,1024]{1,0:T(8,128)(2,1)S(1)} %add_convert_fusion.2), channel_id=1, source_target_pairs={{0,8},{8,16},{16,24},{24,0},{1,9},{9,17},{17,25},{25,1},{2,10},{10... | collective-permute-start | bytes 2359304 | tf_op jit(solution)/shard_map/ppermute | solution.py:65
  (132 other events, 1641.0 us)
Sparse Core Ops, SparseCore 0:
  10.3 119.9 all-gather.2
  132.5 56.4 all-gather.4
  597.2 128.1 all-reduce.3
  796.7 72.5 reduce-scatter.1
